TPU v7x, 256 devices: a whole 4x4x8 slice. The times are simulated.
256 devices in a mesh: cell: 8 (over z_hi, x), seq: 32 (over z_lo, y, core).
Axes of the slice: x: 4, y: 4, z: 8 (z_hi: 2, z_lo: 4; z = z_hi * 4 + z_lo), core: 2. Of those that a mesh axis runs over, the one named last changes fastest.
Arguments:
- features: bfloat16 [8192, 1536], P('seq', 'cell'), may hold values from -6 to 6
- w_qkv: bfloat16 [1536, 768], replicated, may hold values from -0.15625 to 0.15625
- buckets: int32 [8, 64, 16], P('cell', 'seq'), may hold values from 0 to 31
- cell_ids: int32 [8], P('cell'), may hold values from 0 to 31
- bias_table: float32 [32, 32, 2], replicated, may hold values from -8 to 330
- d_attended: bfloat16 [8, 8192, 256], P('cell', 'seq'), may hold values from -6 to 6
Outputs:
- attended: bfloat16 [8, 8192, 256], P('cell', 'seq')
- grad_qkv: float32 [1536, 768], P('cell')
- grad_table: float32 [32, 32, 2], replicated
All inputs are finite; a program needn't handle non-finite values.
Results may differ from a plain program's by a relative error of at most 0.02.
Values may be sent and summed in bfloat16 or wider, within the bound.
A program may use at most 64 MiB of HBM per device.

v0:
```python
import math

import jax
import jax.numpy as jnp
from jax import lax
from jax.sharding import PartitionSpec as P

HEADS = 2
HD = 128
TILE = 128
BT = 16


def passed_along(block, axis, distance):
    devices = range(lax.axis_size(axis))
    route = [(i - distance, i) for i in devices if i - distance in devices]
    return lax.ppermute(block, axis, route)


def tile_bias(bucket_rows, table_row, query_tiles, key_first, key_count, tile_total):
    band_width = bucket_rows.shape[1]
    middle = band_width // 2
    key_tiles = (key_first + jnp.arange(key_count, dtype=jnp.int32)) // TILE
    offsets = key_tiles[None, :] - query_tiles[:, None] + middle
    key_valid = (key_tiles >= 0) & (key_tiles < tile_total)
    query_valid = (query_tiles >= 0) & (query_tiles < tile_total)
    inside = (offsets >= 0) & (offsets < band_width) & key_valid[None, :] & query_valid[:, None]
    matches = offsets[:, :, None] == jnp.arange(band_width, dtype=jnp.int32)[None, None, :]
    bucket_ids = jnp.sum(jnp.where(matches, bucket_rows[:, None, :], 0), axis=2)
    levels = table_row.shape[0]
    onehot = (bucket_ids[:, :, None] == jnp.arange(levels, dtype=jnp.int32)[None, None, :]).astype(
        jnp.float32
    )
    bias_terms = jnp.einsum("qkb,bh->qhk", onehot, table_row, precision=lax.Precision.HIGHEST)
    return (bias_terms, inside, onehot)


def band_scores(query_rows, key_rows, bias_terms, inside, factor):
    raw_scores = jnp.einsum(
        "qhd,khd->qhk", query_rows, key_rows, preferred_element_type=jnp.float32
    )
    tile_count = bias_terms.shape[0]
    shaped = raw_scores.reshape(tile_count, TILE, raw_scores.shape[1], raw_scores.shape[2]) * factor
    shaped = shaped + bias_terms[:, None]
    keep_mask = jnp.broadcast_to(inside[:, None, None, :], shaped.shape)
    shaped = jnp.where(keep_mask, shaped, -1e30)
    return (shaped.reshape(raw_scores.shape), keep_mask.reshape(raw_scores.shape))


def fetch_keys(block, offset):
    return passed_along(block, "seq", -offset)


def return_grads(block, offset):
    return passed_along(block, "seq", offset)


def local(features, w_qkv, buckets, cell_ids, bias_table, d_attended):
    row_count = features.shape[0]
    width_part = features.shape[1]
    inner_width = HEADS * HD
    seq_count = lax.axis_size("seq")
    total_rows = row_count * seq_count
    tile_total = total_rows // TILE
    factor = 1.0 / math.sqrt(HD)
    seq_pos = lax.axis_index("seq")
    tiles_here = row_count // TILE
    half_band = BT * TILE // 2
    reach = min((half_band + row_count - 1) // row_count, seq_count - 1)
    span = 2 * reach + 1
    window_first = (seq_pos - reach) * row_count
    query_tiles = seq_pos * tiles_here + jnp.arange(tiles_here, dtype=jnp.int32)
    cell_pos = lax.axis_index("cell")
    weight_rows = lax.dynamic_slice_in_dim(w_qkv, cell_pos * width_part, width_part, 0)
    partial_qkv = jnp.dot(features, weight_rows, preferred_element_type=jnp.float32)
    projected = lax.psum(partial_qkv, "cell").astype(jnp.bfloat16)
    queries_flat = projected[:, :inner_width]
    queries = queries_flat.reshape(row_count, HEADS, HD)
    queries_wide = queries.astype(jnp.float32)
    key_value = projected[:, inner_width:]
    window_pieces = []
    for offset in range(-reach, reach + 1):
        if offset == 0:
            window_pieces.append(key_value)
        else:
            window_pieces.append(fetch_keys(key_value, offset))
    window_kv = jnp.concatenate(window_pieces, axis=0)
    window_keys = window_kv[:, :inner_width].reshape(span * row_count, HEADS, HD)
    window_values = window_kv[:, inner_width:].reshape(span * row_count, HEADS, HD)
    type_hit = jnp.arange(bias_table.shape[0], dtype=jnp.int32) == cell_ids[0]
    table_row = jnp.sum(jnp.where(type_hit[:, None, None], bias_table, 0.0), axis=0)
    bucket_rows = buckets[0]

    def block_terms(block_index):
        local_first = block_index * row_count
        key_blk = lax.dynamic_slice_in_dim(window_keys, local_first, row_count, 0)
        value_blk = lax.dynamic_slice_in_dim(window_values, local_first, row_count, 0)
        bias_terms, inside, onehot = tile_bias(
            bucket_rows, table_row, query_tiles, window_first + local_first, row_count, tile_total
        )
        scores, keep_mask = band_scores(queries, key_blk, bias_terms, inside, factor)
        return (key_blk, value_blk, scores, keep_mask, onehot)

    def stats_step(block_index, loop_carry):
        row_top, row_mass = loop_carry
        scores, keep_mask = block_terms(block_index)[2:4]
        new_top = jnp.maximum(row_top, jnp.max(scores, axis=2))
        fresh = jnp.sum(jnp.where(keep_mask, jnp.exp(scores - new_top[:, :, None]), 0.0), axis=2)
        return (new_top, row_mass * jnp.exp(row_top - new_top) + fresh)

    start_top = jnp.full((row_count, HEADS), -1e30, jnp.float32)
    start_mass = jnp.zeros((row_count, HEADS), jnp.float32)
    row_top, row_mass = lax.fori_loop(0, span, stats_step, (start_top, start_mass))
    log_total = row_top + jnp.log(row_mass)

    def value_step(block_index, value_sum):
        value_blk, scores, keep_mask = block_terms(block_index)[1:4]
        weights = jnp.where(keep_mask, jnp.exp(scores - log_total[:, :, None]), 0.0).astype(
            jnp.bfloat16
        )
        return value_sum + jnp.einsum(
            "qhk,khd->qhd", weights, value_blk, preferred_element_type=jnp.float32
        )

    value_sum = lax.fori_loop(0, span, value_step, jnp.zeros((row_count, HEADS, HD), jnp.float32))
    attended = value_sum.astype(jnp.bfloat16)
    grad_flat = d_attended[0]
    grad_out = grad_flat.reshape(row_count, HEADS, HD)
    row_delta = jnp.sum(grad_out.astype(jnp.float32) * attended.astype(jnp.float32), axis=2)
    levels = bias_table.shape[1]

    def grad_core(block_index):
        key_blk, value_blk, scores, keep_mask, onehot = block_terms(block_index)
        chance = jnp.where(keep_mask, jnp.exp(scores - log_total[:, :, None]), 0.0)
        chance_b = chance.astype(jnp.bfloat16)
        grad_push = jnp.einsum(
            "qhd,khd->qhk", grad_out, value_blk, preferred_element_type=jnp.float32
        )
        dscore = chance * (grad_push - row_delta[:, :, None])
        q_part = jnp.einsum(
            "qhk,khd->qhd",
            dscore,
            key_blk.astype(jnp.float32),
            precision=lax.Precision.HIGHEST,
            preferred_element_type=jnp.float32,
        )
        tile_sum = dscore.reshape(tiles_here, TILE, HEADS, row_count).sum(axis=1)
        table_part = jnp.einsum("qhk,qkb->bh", tile_sum, onehot, precision=lax.Precision.HIGHEST)
        return (chance_b, dscore, q_part, table_part)

    zero_rows = jnp.zeros((row_count, HEADS, HD), jnp.float32)
    zero_table = jnp.zeros((levels, HEADS), jnp.float32)

    def grad_step(block_index, loop_carry):
        q_total, table_total, key_store = loop_carry
        chance_b, dscore, q_part, table_part = grad_core(block_index)
        key_part = (
            jnp.einsum(
                "qhk,qhd->khd",
                dscore,
                queries_wide,
                precision=lax.Precision.HIGHEST,
                preferred_element_type=jnp.float32,
            )
            * factor
        )
        value_part = jnp.einsum(
            "qhk,qhd->khd", chance_b, grad_out, preferred_element_type=jnp.float32
        )
        merged = jnp.concatenate(
            [key_part.reshape(row_count, inner_width), value_part.reshape(row_count, inner_width)],
            axis=1,
        )
        key_store = lax.dynamic_update_slice_in_dim(key_store, merged, block_index * row_count, 0)
        return (q_total + q_part, table_total + table_part, key_store)

    key_store = jnp.zeros((span * row_count, 2 * inner_width), jnp.float32)
    q_total, table_total, key_store = lax.fori_loop(
        0, span, grad_step, (zero_rows, zero_table, key_store)
    )
    key_grads = key_store[reach * row_count : (reach + 1) * row_count]
    for slot_index in range(span):
        offset = slot_index - reach
        if offset != 0:
            segment = key_store[slot_index * row_count : (slot_index + 1) * row_count]
            key_grads = key_grads + return_grads(segment, offset)
    query_grads = (q_total * factor).reshape(row_count, inner_width)
    row_grads = jnp.concatenate([query_grads, key_grads], axis=1)
    summed_rows = lax.psum(row_grads, "cell")
    share = jnp.dot(
        features.astype(jnp.float32).T,
        summed_rows,
        precision=lax.Precision.HIGHEST,
        preferred_element_type=jnp.float32,
    )
    grad_qkv = lax.psum(share, "seq")
    table_term = jnp.where(type_hit[:, None, None], table_total[None, :, :], 0.0)
    grad_table = lax.psum(table_term, ("cell", "seq"))
    return (attended.reshape(1, row_count, inner_width), grad_qkv, grad_table)


def solution(mesh):
    in_specs = (
        P("seq", "cell"),
        P(),
        P("cell", "seq", None),
        P("cell"),
        P(),
        P("cell", "seq", None),
    )
    out_specs = (P("cell", "seq", None), P("cell", None), P())
    return jax.shard_map(local, mesh=mesh, in_specs=in_specs, out_specs=out_specs, check_vma=False)
```

profile of v0, /device:TPU:1, one launch (start us, length us, event | category | flops | bytes accessed | tf_op | source)
XLA Modules:
  0.0 757.1 jit_solution(12148896757726910611)
XLA Ops:
  7.3 1.6 copy-done
  10.0 61.8 %all-reduce.7 = bf16[256,768]{0,1:T(8,128)(2,1)} all-reduce(f32[256,768]{0,1:T(8,128)S(1)} %convolution_bitcast_fusion.6), channel_id=1, replica_groups=mesh['cell'=8,'seq'=32] {'cell'}, use_global_device_ids=true, to_apply=%region_0.0 | all-reduce | flops 196608 | bytes 1179648 | tf_op jit(solution)/shard_map/psum | solution.py:76
  72.9 5.5 collective-permute-start
  81.0 14.5 %collective-permute-start.2 = (bf16[256,512]{0,1:T(8,128)(2,1)S(1)}, bf16[256,512]{0,1:T(8,128)(2,1)}, u32[]{:S(2)}, u32[]{:S(2)}) collective-permute-start(bf16[256,512]{0,1:T(8,128)(2,1)S(1)} %slice.52), channel_id=1, source_target_pairs={{0,2},{1,3},{2,4},{3,5},{4,6},{5,7},{6,8},{7,9},{8,10},{9,11},{10,... | collective-permute-start | bytes 786440 | tf_op jit(solution)/shard_map/ppermute | solution.py:17
  95.5 5.6 collective-permute-start.1
  105.0 2.0 collective-permute-start.3
  110.4 2.3 collective-permute-start.4
  113.7 7.9 %collective-permute-done.4 = bf16[256,512]{0,1:T(8,128)(2,1)S(1)} collective-permute-done((bf16[256,512]{0,1:T(8,128)(2,1)S(1)}, bf16[256,512]{0,1:T(8,128)(2,1)S(1)}, u32[]{:S(2)}, u32[]{:S(2)}) %collective-permute-start.4) | collective-permute-done | bytes 262176 | tf_op jit(solution)/shard_map/ppermute | solution.py:17
  122.7 1.6 fusion.66
  124.3 2.4 copy.86
  126.7 48.4 %while.54 = (s32[]{:T(128)}, f32[256,2]{0,1:T(2,128)S(1)}, f32[256,2]{0,1:T(2,128)S(1)}, s32[]{:T(128)}, bf16[2304,2,128]{2,0,1:T(8,128)(2,1)}, /*index=5*/bf16[...) while((s32[]{:T(128)}, f32[256,2]{0,1:T(2,128)S(1)}, ...), condition=%wide.region_6.7_spmd.clone, body=%wide.region_2.6_spmd.clone.sunk | while | flops 34921744 | bytes 3791994 | solution.py:113
  175.1 51.4 %while.55 = (s32[]{:T(128)}, f32[256,2,128]{0,2,1:T(8,128)}, bf16[2304,2,128]{0,2,1:T(8,128)(2,1)}, s32[]{:T(128)}, bf16[2304,2,128]{2,0,1:T(8,128)(2,1)}, /*ind...) while((s32[]{:T(128)}, f32[256,2,128]{0,2,1:T(8,128)}, ...), condition=%wide.region_9.10_spmd.clone, body=%wide.region_7.9_spmd.clone.sunk | while | flops 68473616 | bytes 3834520 | solution.py:125
  178.4 2.4 fusion.112
  184.1 2.4 fusion.112
  189.8 2.4 fusion.112
  195.5 2.4 fusion.112
  201.2 2.4 fusion.112
  206.9 2.4 fusion.112
  212.6 2.4 fusion.112
  218.4 2.4 fusion.112
  224.1 2.4 fusion.112
  227.5 2.4 broadcast_in_dim.354
  230.0 60.5 %while.56 = (s32[]{:T(128)}, f32[256,2,128]{0,2,1:T(8,128)S(1)}, f32[32,2]{0,1:T(2,128)S(1)}, f32[2304,512]{0,1:T(8,128)}, bf16[2304,2,128]{2,0,1:T(8,128)(2,1)}...) while((s32[]{:T(128)}, f32[256,2,128]{0,2,1:T(8,128)S(1)}, ...), condition=%wide.region_14.15_spmd.clone, body=%wide.region_11.14_spmd.clone.sunk | while | flops 505679744 | bytes 7515830 | solution.py:178
  234.0 1.4 fusion.125
  240.7 1.4 fusion.125
  247.5 1.4 fusion.125
  254.2 1.4 fusion.125
  260.9 1.4 fusion.125
  267.6 1.4 fusion.125
  274.3 1.4 fusion.125
  281.0 1.4 fusion.125
  287.8 1.4 fusion.125
  290.5 2.6 fusion.65
  294.4 3.5 collective-permute-start.13
  297.9 2.6 collective-permute-start.12
  300.6 1.9 collective-permute-start.11
  303.8 6.5 collective-permute-done.8
  311.6 8.1 %collective-permute-done.13 = f32[256,512]{0,1:T(8,128)S(1)} collective-permute-done((f32[256,512]{0,1:T(8,128)S(1)}, f32[256,512]{0,1:T(8,128)S(1)}, u32[]{:S(2)}, u32[]{:S(2)}) %collective-permute-start.13) | collective-permute-done | bytes 524320 | tf_op jit(solution)/shard_map/ppermute | solution.py:17
  319.7 6.6 collective-permute-start.15
  326.4 5.9 collective-permute-start.14
  332.3 5.5 collective-permute-done.15
  337.8 16.9 %collective-permute-done.14 = f32[256,512]{0,1:T(8,128)S(1)} collective-permute-done((f32[256,512]{0,1:T(8,128)S(1)}, f32[256,512]{0,1:T(8,128)S(1)}, u32[]{:S(2)}, u32[]{:S(2)}) %collective-permute-start.14) | collective-permute-done | bytes 524320 | tf_op jit(solution)/shard_map/ppermute | solution.py:17
  354.7 1.4 add_add_fusion
  357.1 119.5 %all-reduce.4.cloned.1.call-done = f32[256,768]{0,1:T(8,128)} async-done(((f32[256,768]{0,1:T(8,128)}), f32[256,768]{0,1:T(8,128)}) %all-reduce.4.cloned.1.call-update) | async-done | bytes 786448 | tf_op jit(solution)/shard_map/psum | solution.py:189
  476.6 2.5 convolution_bitcast_fusion.7
  480.0 79.9 %psum.31 = f32[32,32,2]{1,2,0:T(2,128)} all-reduce(f32[32,32,2]{1,2,0:T(2,128)S(1)} %broadcast_select_fusion.1), channel_id=1, replica_groups=mesh['cell'=8,'seq'=32] {'cell','seq'}, use_global_device_ids=true, to_apply=%region_17.18 | all-reduce | flops 2048 | bytes 16384 | tf_op jit(solution)/shard_map/psum | solution.py:198
  560.0 188.4 %all-reduce.6.cloned.1.call-done = f32[192,768]{1,0:T(8,128)} async-done(((f32[192,768]{1,0:T(8,128)}), f32[192,768]{1,0:T(8,128)}) %all-reduce.6.cloned.1.call-update) | async-done | bytes 589840 | tf_op jit(solution)/shard_map/psum | solution.py:196
  748.4 1.9 copy.153
  (518 shorter events, 144.3 us)
Async XLA Ops:
  7.2 1.7 copy-start
  7.2 94.6 %copy-start.9 = (f32[32,32,2]{1,2,0:T(2,128)S(1)}, f32[32,32,2]{1,2,0:T(2,128)}, u32[]{:S(2)}) copy-start(f32[32,32,2]{1,2,0:T(2,128)} %param.16) | copy-start | bytes 24580
  7.2 97.7 %copy-start.8 = (bf16[1,256,256]{2,1,0:T(8,128)(2,1)S(1)}, bf16[1,256,256]{2,1,0:T(8,128)(2,1)}, u32[]{:S(2)}) copy-start(bf16[1,256,256]{2,1,0:T(8,128)(2,1)} %param.17) | copy-start | bytes 393220
  7.2 469.4 %all-reduce.4.cloned.1.call-start = ((), (), s32[]{:S(2)}) async-start(), calls=%async_computation | async-start | bytes 1572864 | tf_op jit(solution)/shard_map/psum | solution.py:189
  71.9 41.8 %copy-start.5 = (bf16[256,768]{0,1:T(8,128)(2,1)S(1)}, bf16[256,768]{0,1:T(8,128)(2,1)}, u32[]{:S(2)}) copy-start(bf16[256,768]{0,1:T(8,128)(2,1)} %all-reduce.7) | copy-start | bytes 1179652
  72.9 32.1 %collective-permute-start = (bf16[256,512]{0,1:T(8,128)(2,1)S(1)}, bf16[256,512]{0,1:T(8,128)(2,1)}, u32[]{:S(2)}, u32[]{:S(2)}) collective-permute-start(bf16[256,512]{0,1:T(8,128)(2,1)S(1)} %slice.52), channel_id=1, source_target_pairs={{0,4},{1,5},{2,6},{3,7},{4,8},{5,9},{6,10},{7,11},{8,12},{9,13},{1... | collective-permute-start | bytes 786440 | tf_op jit(solution)/shard_map/ppermute | solution.py:17
  78.5 44.2 %collective-permute-start.7 = (bf16[256,512]{0,1:T(8,128)(2,1)S(1)}, bf16[256,512]{0,1:T(8,128)(2,1)S(1)}, u32[]{:S(2)}, u32[]{:S(2)}) collective-permute-start(bf16[256,512]{0,1:T(8,128)(2,1)S(1)} %slice.52), channel_id=1, source_target_pairs={{4,0},{5,1},{6,2},{7,3},{8,4},{9,5},{10,6},{11,7},{12,8},{13,9},{1... | collective-permute-start | bytes 786440 | tf_op jit(solution)/shard_map/ppermute | solution.py:17
  79.8 41.9 %collective-permute-start.6 = (bf16[256,512]{0,1:T(8,128)(2,1)S(1)}, bf16[256,512]{0,1:T(8,128)(2,1)}, u32[]{:S(2)}, u32[]{:S(2)}) collective-permute-start(bf16[256,512]{0,1:T(8,128)(2,1)S(1)} %slice.52), channel_id=1, source_target_pairs={{3,0},{4,1},{5,2},{6,3},{7,4},{8,5},{9,6},{10,7},{11,8},{12,9},{13... | collective-permute-start | bytes 786440 | tf_op jit(solution)/shard_map/ppermute | solution.py:17
  81.0 29.3 %collective-permute-start.2 = (bf16[256,512]{0,1:T(8,128)(2,1)S(1)}, bf16[256,512]{0,1:T(8,128)(2,1)}, u32[]{:S(2)}, u32[]{:S(2)}) collective-permute-start(bf16[256,512]{0,1:T(8,128)(2,1)S(1)} %slice.52), channel_id=1, source_target_pairs={{0,2},{1,3},{2,4},{3,5},{4,6},{5,7},{6,8},{7,9},{8,10},{9,11},{10,... | collective-permute-start | bytes 786440 | tf_op jit(solution)/shard_map/ppermute | solution.py:17
  95.5 12.6 %collective-permute-start.1 = (bf16[256,512]{0,1:T(8,128)(2,1)S(1)}, bf16[256,512]{0,1:T(8,128)(2,1)}, u32[]{:S(2)}, u32[]{:S(2)}) collective-permute-start(bf16[256,512]{0,1:T(8,128)(2,1)S(1)} %slice.52), channel_id=1, source_target_pairs={{0,3},{1,4},{2,5},{3,6},{4,7},{5,8},{6,9},{7,10},{8,11},{9,12},{10... | collective-permute-start | bytes 786440 | tf_op jit(solution)/shard_map/ppermute | solution.py:17
  105.0 8.6 %collective-permute-start.3 = (bf16[256,512]{0,1:T(8,128)(2,1)S(1)}, bf16[256,512]{0,1:T(8,128)(2,1)S(1)}, u32[]{:S(2)}, u32[]{:S(2)}) collective-permute-start(bf16[256,512]{0,1:T(8,128)(2,1)S(1)} %slice.52), channel_id=1, source_target_pairs={{0,1},{1,2},{2,3},{3,4},{4,5},{5,6},{6,7},{7,8},{8,9},{9,10},{10,1... | collective-permute-start | bytes 786440 | tf_op jit(solution)/shard_map/ppermute | solution.py:17
  108.1 13.5 %collective-permute-start.5 = (bf16[256,512]{0,1:T(8,128)(2,1)S(1)}, bf16[256,512]{0,1:T(8,128)(2,1)S(1)}, u32[]{:S(2)}, u32[]{:S(2)}) collective-permute-start(bf16[256,512]{0,1:T(8,128)(2,1)S(1)} %slice.52), channel_id=1, source_target_pairs={{2,0},{3,1},{4,2},{5,3},{6,4},{7,5},{8,6},{9,7},{10,8},{11,9},{12,... | collective-permute-start | bytes 786440 | tf_op jit(solution)/shard_map/ppermute | solution.py:17
  110.4 11.3 %collective-permute-start.4 = (bf16[256,512]{0,1:T(8,128)(2,1)S(1)}, bf16[256,512]{0,1:T(8,128)(2,1)S(1)}, u32[]{:S(2)}, u32[]{:S(2)}) collective-permute-start(bf16[256,512]{0,1:T(8,128)(2,1)S(1)} %slice.52), channel_id=1, source_target_pairs={{1,0},{2,1},{3,2},{4,3},{5,4},{6,5},{7,6},{8,7},{9,8},{10,9},{11,1... | collective-permute-start | bytes 786440 | tf_op jit(solution)/shard_map/ppermute | solution.py:17
  124.3 2.4 copy-start.7
  175.1 3.3 copy-start.1
  180.8 3.3 copy-start.1
  186.5 3.3 copy-start.1
  192.2 3.3 copy-start.1
  197.9 3.3 copy-start.1
  203.6 3.3 copy-start.1
  209.3 3.3 copy-start.1
  215.1 3.3 copy-start.1
  220.8 3.3 copy-start.1
  227.5 2.5 copy-start.2
  227.5 2.5 copy-start.3
  227.5 2.5 copy-start.4
  227.5 2.5 copy-start.10
  293.1 17.2 %collective-permute-start.8 = (f32[256,512]{0,1:T(8,128)S(1)}, f32[256,512]{0,1:T(8,128)S(1)}, u32[]{:S(2)}, u32[]{:S(2)}) collective-permute-start(f32[256,512]{0,1:T(8,128)S(1)} %get-tuple-element.1193), channel_id=1, source_target_pairs={{4,0},{5,1},{6,2},{7,3},{8,4},{9,5},{10,6},{11,7},{12,8},{13,9},{1... | collective-permute-start | bytes 1572872 | tf_op jit(solution)/shard_map/ppermute | solution.py:17
  294.4 25.3 %collective-permute-start.13 = (f32[256,512]{0,1:T(8,128)S(1)}, f32[256,512]{0,1:T(8,128)S(1)}, u32[]{:S(2)}, u32[]{:S(2)}) collective-permute-start(f32[256,512]{0,1:T(8,128)S(1)} %get-tuple-element.1194), channel_id=1, source_target_pairs={{0,2},{1,3},{2,4},{3,5},{4,6},{5,7},{6,8},{7,9},{8,10},{9,11},{10,... | collective-permute-start | bytes 1572872 | tf_op jit(solution)/shard_map/ppermute | solution.py:17
  297.9 28.4 %collective-permute-start.12 = (f32[256,512]{0,1:T(8,128)S(1)}, f32[256,512]{0,1:T(8,128)S(1)}, u32[]{:S(2)}, u32[]{:S(2)}) collective-permute-start(f32[256,512]{0,1:T(8,128)S(1)} %get-tuple-element.1195), channel_id=1, source_target_pairs={{0,1},{1,2},{2,3},{3,4},{4,5},{5,6},{6,7},{7,8},{8,9},{9,10},{10,1... | collective-permute-start | bytes 1572872 | tf_op jit(solution)/shard_map/ppermute | solution.py:17
  300.6 31.7 %collective-permute-start.11 = (f32[256,512]{0,1:T(8,128)S(1)}, f32[256,512]{0,1:T(8,128)S(1)}, u32[]{:S(2)}, u32[]{:S(2)}) collective-permute-start(f32[256,512]{0,1:T(8,128)S(1)} %get-tuple-element.1196), channel_id=1, source_target_pairs={{1,0},{2,1},{3,2},{4,3},{5,4},{6,5},{7,6},{8,7},{9,8},{10,9},{11,1... | collective-permute-start | bytes 1572872 | tf_op jit(solution)/shard_map/ppermute | solution.py:17
  302.5 29.8 %collective-permute-start.10 = (f32[256,512]{0,1:T(8,128)S(1)}, f32[256,512]{0,1:T(8,128)S(1)}, u32[]{:S(2)}, u32[]{:S(2)}) collective-permute-start(f32[256,512]{0,1:T(8,128)S(1)} %get-tuple-element.1197), channel_id=1, source_target_pairs={{2,0},{3,1},{4,2},{5,3},{6,4},{7,5},{8,6},{9,7},{10,8},{11,9},{12,... | collective-permute-start | bytes 1572872 | tf_op jit(solution)/shard_map/ppermute | solution.py:17
  310.3 22.0 %collective-permute-start.9 = (f32[256,512]{0,1:T(8,128)S(1)}, f32[256,512]{0,1:T(8,128)S(1)}, u32[]{:S(2)}, u32[]{:S(2)}) collective-permute-start(f32[256,512]{0,1:T(8,128)S(1)} %get-tuple-element.1198), channel_id=1, source_target_pairs={{3,0},{4,1},{5,2},{6,3},{7,4},{8,5},{9,6},{10,7},{11,8},{12,9},{13... | collective-permute-start | bytes 1572872 | tf_op jit(solution)/shard_map/ppermute | solution.py:17
  319.7 18.1 %collective-permute-start.15 = (f32[256,512]{0,1:T(8,128)S(1)}, f32[256,512]{0,1:T(8,128)S(1)}, u32[]{:S(2)}, u32[]{:S(2)}) collective-permute-start(f32[256,512]{0,1:T(8,128)S(1)} %get-tuple-element.1199), channel_id=1, source_target_pairs={{0,4},{1,5},{2,6},{3,7},{4,8},{5,9},{6,10},{7,11},{8,12},{9,13},{1... | collective-permute-start | bytes 1572872 | tf_op jit(solution)/shard_map/ppermute | solution.py:17
  326.4 28.3 %collective-permute-start.14 = (f32[256,512]{0,1:T(8,128)S(1)}, f32[256,512]{0,1:T(8,128)S(1)}, u32[]{:S(2)}, u32[]{:S(2)}) collective-permute-start(f32[256,512]{0,1:T(8,128)S(1)} %get-tuple-element.1200), channel_id=1, source_target_pairs={{0,3},{1,4},{2,5},{3,6},{4,7},{5,8},{6,9},{7,10},{8,11},{9,12},{10... | collective-permute-start | bytes 1572872 | tf_op jit(solution)/shard_map/ppermute | solution.py:17
  356.0 120.6 %copy-start.6 = (bf16[256,192]{0,1:T(8,128)(2,1)S(1)}, bf16[256,192]{0,1:T(8,128)(2,1)}, u32[]{:S(2)}) copy-start(bf16[256,192]{0,1:T(8,128)(2,1)} %param.12) | copy-start | bytes 294916
  357.0 391.3 %all-reduce.6.cloned.1.call-start = ((), (), s32[]{:S(2)}) async-start(), calls=%async_computation.1 | async-start | bytes 1179648 | tf_op jit(solution)/shard_map/psum | solution.py:196
Sparse Core Ops, SparseCore 0:
  357.2 119.4 all-reduce.3
  479.8 268.5 all-reduce.5
where the time goes:
time: 761 us; the launch traced here: 757 us
  waiting for transfers between devices  353 us (46%)
  blocking collectives  142 us (19%)
  matrix products  100 us (13%)
  starting transfers between devices  58.3 us (8%)
  local copies, waits for them, and re-layouts  57.9 us (8%)
  other arithmetic  29 us (4%)
  between operations  15.1 us (2%)
    psum x1, waiting for transfers between devices, local(): grad_qkv = lax.psum(share, 'seq')  188 us
    psum x1, waiting for transfers between devices, local(): summed_rows = lax.psum(row_grads, 'cell')  120 us
    psum x1, blocking collectives, local(): grad_table = lax.psum(table_term, ('cell', 'seq'))  79.9 us
    psum x1, blocking collectives, local(): projected = lax.psum(partial_qkv, 'cell').astype(jnp.bfloat16)  61.8 us
    ppermute x16, starting transfers between devices, passed_along(): return lax.ppermute(block, axis, route)  58.2 us
    ppermute x16, waiting for transfers between devices, passed_along(): return lax.ppermute(block, axis, route)  45 us
    add x45, local copies, waits for them, and re-layouts, band_scores(): shaped = shaped + bias_terms[:, None]  26.1 us
    dot_general x18, matrix products, band_scores(): jnp.einsum('qhd,khd->qhk', query_rows, key_rows, preferred_element_type=j...  22.1 us
  transfers between devices with their start and end apart: 18, of which 8 were waited for; matrix products, arithmetic and copies ran while one was open for 1% of the time, Pallas kernels for 0%

commit v1 on v0

v1 whole, which is shorter than its diff:
```python
import math

import jax
import jax.numpy as jnp
from jax import lax
from jax.experimental import pallas as pl
from jax.experimental.pallas import tpu as pltpu
from jax.sharding import PartitionSpec as P

HEADS = 2
HD = 128
TILE = 128
BT = 16
NSEQ = 32
NWIN = 17
TPAD = 24
NEG = -1e30
FACTOR = 1.0 / math.sqrt(HD)
F32 = jnp.float32
BF16 = jnp.bfloat16

S_FEAT = 0
S_FCROSS = 7
S_DO = 8
S_BIAS = 11
S_KV = 14
S_Q = 17
S_WIN = 18
S_ATT = 26
S_TT = 29
S_DKV = 32
S_XKV = 40
S_XQ = 43
S_GC = 46
S_TC = 47
S_GY = 48
S_TY = 51
S_GZ = 54
S_TZ = 61
S_TX = 68
S_OY = 71
S_OC = 74
N_SEM = 75

WIN_OFFSETS = (-4, 4, -3, 3, -2, 2, -1, 1)


def dot_nn(a, b):
    return lax.dot_general(a, b, (((1,), (0,)), ((), ())), preferred_element_type=F32)


def dot_nt(a, b):
    return lax.dot_general(a, b, (((1,), (1,)), ((), ())), preferred_element_type=F32)


def dot_tn(a, b):
    return lax.dot_general(a, b, (((0,), (0,)), ((), ())), preferred_element_type=F32)


def kernel(
    feat_ref, w_hbm, bias_ref, oht_ref, hit_ref, dout_ref,
    att_out, grad_out, table_out,
    w_ref, fbuf, fcross, dot_src, dot_buf, bias_buf, proj_kv, proj_q, q_buf, kvw,
    e0_buf, o_buf, m_buf, l_buf, d_buf, w_buf, dof_buf,
    att_src, att_buf, tt_src, tt_buf, dkvw, dkv_in, dkv_x, dq_x, d3,
    g_src, g_core, g_c, g_y, g_zs, g_z, g_oy, g_oc,
    t_c, t_y, t_z, t_x, w_sem, send_sem, recv_sem,
):
    cell = lax.axis_index("cell")
    seq = lax.axis_index("seq")
    zh = cell // 4
    x = cell % 4
    z_lo = seq // 8
    y = (seq // 2) % 4
    core = seq % 2
    zi = zh * 4 + z_lo
    head = x % 2
    half = x // 2

    def at_x(k):
        return (zh * 4 + (x + k) % 4, seq)

    def at_cross(k):
        return ((1 - zh) * 4 + (x + k) % 4, seq)

    def at_seq(o):
        return (cell, (seq + o + NSEQ) % NSEQ)

    def at_y(k):
        return (cell, z_lo * 8 + ((y + k) % 4) * 2 + core)

    def at_z(k):
        there = (zi + k) % 8
        return ((there // 4) * 4 + x, (there % 4) * 8 + y * 2 + core)

    sibling = (cell, seq + 1 - 2 * core)

    w_copy = pltpu.make_async_copy(w_hbm, w_ref, w_sem)
    w_copy.start()

    barrier = pltpu.get_barrier_semaphore()
    greet = [at_cross(k) for k in range(4)] + [at_x(k) for k in (1, 2, 3)]
    greet += [at_seq(o) for o in WIN_OFFSETS]
    greet += [at_y(k) for k in (1, 2, 3)] + [at_z(k) for k in range(1, 8)]
    for peer in greet:
        pl.semaphore_signal(barrier, inc=1, device_id=peer, device_id_type=pl.DeviceIdType.MESH)

    sends = []

    def remote(src, dst, slot, peer):
        copy = pltpu.make_async_remote_copy(
            src_ref=src,
            dst_ref=dst,
            send_sem=send_sem.at[slot],
            recv_sem=recv_sem.at[slot],
            device_id=peer,
            device_id_type=pl.DeviceIdType.MESH,
        )
        copy.start()
        sends.append(copy)
        return copy

    for piece in range(4):
        r, h = piece // 2, piece % 2
        block = dout_ref[128 * r : 128 * r + 128, 128 * h : 128 * h + 128]
        dot_src[piece] = block.astype(F32).T.astype(BF16)

    pl.semaphore_wait(barrier, len(greet))

    feat_in = []
    for k in range(4):
        there = (x + k) % 4
        feat_in.append(
            remote(feat_ref.at[pl.ds(64 * there, 64)], fbuf.at[cell], S_FEAT + k, at_cross(k))
        )
    for k in (1, 2, 3):
        there = (x + k) % 4
        feat_in.append(
            remote(feat_ref.at[pl.ds(64 * there, 64)], fbuf.at[cell], S_FEAT + 3 + k, at_x(k))
        )
    do_in = []
    bias_in = []
    for k in (1, 2, 3):
        there = (x + k) % 4
        do_in.append(remote(dot_src.at[there], dot_buf.at[x], S_DO + k - 1, at_x(k)))
        bias_in.append(remote(bias_ref.at[there], bias_buf.at[x], S_BIAS + k - 1, at_x(k)))
    cross_in = remote(feat_ref, fcross, S_FCROSS, at_cross(0))

    dot_buf[x] = dot_src[x]
    bias_buf[x] = bias_ref[x]
    fbuf[cell] = feat_ref[pl.ds(64 * x, 64), :]
    w_copy.wait()
    for copy in feat_in:
        copy.wait_recv()

    proj = jnp.zeros((64, 768), F32)
    for c in range(8):
        proj = proj + dot_nn(fbuf[c], w_ref[192 * c : 192 * c + 192, :])
    projected = proj.astype(BF16)
    for h in range(2):
        proj_q[h] = projected[:, 128 * h : 128 * h + 128]
        proj_kv[h, :, 0:128] = projected[:, 256 + 128 * h : 384 + 128 * h]
        proj_kv[h, :, 128:256] = projected[:, 512 + 128 * h : 640 + 128 * h]

    my_tile = 8 + x // 2
    my_rows = pl.ds(64 * (x % 2), 64)
    kv_in = []
    for k in (1, 2, 3):
        there = (x + k) % 4
        kv_in.append(
            remote(proj_kv.at[there % 2], kvw.at[my_tile, my_rows], S_KV + k - 1, at_x(k))
        )
    mate = (zh * 4 + x + 1 - 2 * (x % 2), seq)
    q_in = remote(proj_q.at[1 - head], q_buf.at[my_rows], S_Q, mate)
    kvw[my_tile, my_rows] = proj_kv[head]
    q_buf[my_rows] = proj_q[head]
    for copy in kv_in:
        copy.wait_recv()

    win_in = {}
    for n, o in enumerate(WIN_OFFSETS):
        count = 1 if o == -4 else 2
        win_in[4 - o] = remote(
            kvw.at[pl.ds(8, count)], kvw.at[pl.ds(8 - 2 * o, count)], S_WIN + n, at_seq(o)
        )
    q_in.wait_recv()
    for copy in do_in + bias_in:
        copy.wait_recv()

    q_tile = q_buf[...]
    for c in range(4):
        dof_buf[c] = dot_buf[c].astype(F32)
    m_buf[...] = jnp.zeros((TPAD, 128), F32)
    l_buf[...] = jnp.zeros((TPAD, 128), F32)
    d_buf[...] = jnp.zeros((4, TPAD, 128), F32)

    def forward_tile(t):
        keys = kvw[t, :, 0:128]
        values = kvw[t, :, 128:256]
        s = dot_nt(keys, q_tile) * FACTOR
        top = jnp.max(s, axis=0, keepdims=True)
        e0 = jnp.exp(s - top)
        m_buf[t : t + 1, :] = top
        l_buf[t : t + 1, :] = jnp.sum(e0, axis=0, keepdims=True)
        e0b = e0.astype(BF16)
        e0_buf[t] = e0b
        o_t = dot_tn(values, e0b)
        o_buf[t] = o_t
        for c in range(4):
            d_buf[c, t : t + 1, :] = jnp.sum(dof_buf[c] * o_t, axis=0, keepdims=True)

    for slot in (4, 3, 5, 2, 6, 1, 7, 0, 8):
        if slot != 4:
            win_in[slot].wait_recv()
        forward_tile(2 * slot)
        if slot != 8:
            forward_tile(2 * slot + 1)

    m_all = m_buf[...]
    l_all = l_buf[...]
    big = jnp.zeros((TPAD, 128), F32)
    att_in = []
    tt_in = []
    for c in range(4):
        z = m_all + bias_buf[c]
        top = jnp.max(z, axis=0, keepdims=True)
        ex = jnp.exp(z - top)
        mass = jnp.sum(ex * l_all, axis=0, keepdims=True)
        w_c = ex / mass
        w_buf[c] = w_c
        acc = jnp.zeros((128, 128), F32)
        for t in range(NWIN):
            acc = acc + w_c[t : t + 1, :] * o_buf[t]
        accb = acc.astype(BF16)
        att_src[c] = acc.T.astype(BF16)
        delta = jnp.sum(dof_buf[c] * accb.astype(F32), axis=0, keepdims=True)
        big = big + w_c * delta
        tt_src[c] = w_c * (d_buf[c] - delta * l_all)
    for k in (1, 2, 3):
        there = (x + k) % 4
        att_in.append(remote(att_src.at[there], att_buf.at[x], S_ATT + k - 1, at_x(k)))
        tt_in.append(remote(tt_src.at[there], tt_buf.at[x], S_TT + k - 1, at_x(k)))
    att_buf[x] = att_src[x]
    tt_buf[x] = tt_src[x]

    dq_acc = jnp.zeros((128, 128), F32)
    dkv_get = {}
    for slot in (0, 8, 1, 7, 2, 6, 3, 5, 4):
        for t in (2 * slot, 2 * slot + 1):
            if t >= NWIN:
                continue
            g_t = w_buf[0, t : t + 1, :] * dof_buf[0]
            for c in (1, 2, 3):
                g_t = g_t + w_buf[c, t : t + 1, :] * dof_buf[c]
            gb = g_t.astype(BF16)
            e0b = e0_buf[t]
            dp = dot_nn(kvw[t, :, 128:256], gb)
            ds = (e0b.astype(F32) * (dp - big[t : t + 1, :])).astype(BF16)
            dkvw[t, :, 0:128] = (dot_nn(ds, q_tile) * FACTOR).astype(BF16)
            dkvw[t, :, 128:256] = dot_nt(e0b, gb).astype(BF16)
            dq_acc = dq_acc + dot_tn(ds, kvw[t, :, 0:128])
        o = slot - 4
        if o != 0:
            n = WIN_OFFSETS.index(o)
            count = 1 if o == 4 else 2
            dkv_get[4 - o] = remote(
                dkvw.at[pl.ds(2 * slot, count)],
                dkv_in.at[pl.ds(2 * (4 - o), count)],
                S_DKV + n,
                at_seq(o),
            )
    dq_x[x] = (dq_acc * FACTOR).astype(BF16)
    xq_in = [remote(dq_x.at[x], dq_x.at[x], S_XQ + k - 1, at_x(k)) for k in (1, 2, 3)]

    for copy in tt_in:
        copy.wait_recv()
    ones = jnp.ones((8, 128), F32)
    row = jnp.zeros((8, 128), F32)
    for piece in range(4):
        sums = lax.dot_general(
            ones, tt_buf[piece], (((1,), (1,)), ((), ())),
            precision=lax.Precision.HIGHEST, preferred_element_type=F32,
        )
        row = row + lax.dot_general(
            sums, oht_ref[piece], (((1,), (0,)), ((), ())),
            precision=lax.Precision.HIGHEST, preferred_element_type=F32,
        )
    t_c[core] = hit_ref[...] * row[0:1, :]
    tc_in = remote(t_c.at[core], t_c.at[core], S_TC, sibling)

    for copy in att_in:
        copy.wait_recv()
    for piece in range(4):
        r, h = piece // 2, piece % 2
        att_out[128 * r : 128 * r + 128, 128 * h : 128 * h + 128] = att_buf[piece]

    for slot in (4, 3, 5, 2, 6, 1, 7, 0, 8):
        if slot != 4:
            dkv_get[slot].wait_recv()
    for t in range(2):
        acc = dkvw[8 + t].astype(F32)
        for slot in (3, 5, 2, 6, 1, 7, 0, 8):
            if slot == 0 and t == 1:
                continue
            acc = acc + dkv_in[2 * slot + t].astype(F32)
        dkv_x[x, t] = acc.astype(BF16)
    xkv_in = [remote(dkv_x.at[x], dkv_x.at[x], S_XKV + k - 1, at_x(k)) for k in (1, 2, 3)]

    tc_in.wait_recv()
    t_y[y] = t_c[0] + t_c[1]
    ty_in = [remote(t_y.at[y], t_y.at[y], S_TY + k - 1, at_y(k)) for k in (1, 2, 3)]

    for copy in xq_in + xkv_in:
        copy.wait_recv()
    for t in range(2):
        for h in range(2):
            rows = slice(128 * t, 128 * t + 128)
            d3[rows, 128 * h : 128 * h + 128] = dq_x[2 * t + h]
            both = dkv_x[h, t].astype(F32) + dkv_x[2 + h, t].astype(F32)
            bothb = both.astype(BF16)
            d3[rows, 256 + 128 * h : 384 + 128 * h] = bothb[:, 0:128]
            d3[rows, 512 + 128 * h : 640 + 128 * h] = bothb[:, 128:256]

    cross_in.wait_recv()
    d_all = d3[...]
    own = dot_tn(feat_ref[...], d_all).astype(BF16)
    other = dot_tn(fcross[...], d_all).astype(BF16)
    for k in range(2):
        g_src[k, zh] = own[:, 384 * k : 384 * k + 384]
        g_src[k, 1 - zh] = other[:, 384 * k : 384 * k + 384]
    gc_in = remote(g_src.at[1 - core], g_core, S_GC, sibling)

    for copy in ty_in:
        copy.wait_recv()
    t_z[zi] = (t_y[0] + t_y[1]) + (t_y[2] + t_y[3])
    tz_in = [remote(t_z.at[zi], t_z.at[zi], S_TZ + k - 1, at_z(k)) for k in range(1, 8)]

    gc_in.wait_recv()
    g_c[...] = (g_src[core].astype(F32) + g_core[...].astype(F32)).astype(BF16)
    gy_in = []
    for k in (1, 2, 3):
        there = (y + k) % 4
        gy_in.append(
            remote(g_c.at[:, pl.ds(48 * there, 48)], g_y.at[y], S_GY + k - 1, at_y(k))
        )
    g_y[y] = g_c[:, pl.ds(48 * y, 48), :]

    for copy in tz_in:
        copy.wait_recv()
    total = t_z[0]
    for k in range(1, 8):
        total = total + t_z[k]
    t_x[x] = total
    tx_in = [remote(t_x.at[x], t_x.at[x], S_TX + k - 1, at_x(k)) for k in (1, 2, 3)]

    for copy in gy_in:
        copy.wait_recv()
    piece = g_y[0].astype(F32)
    for k in (1, 2, 3):
        piece = piece + g_y[k].astype(F32)
    g_zs[...] = piece.astype(BF16)
    gz_in = []
    for k in (4, 3, 5, 2, 6, 1, 7):
        there = (zi + k) % 8
        gz_in.append(remote(g_zs.at[there // 4], g_z.at[zi], S_GZ + k - 1, at_z(k)))
    g_z[zi] = g_zs[zh]

    for copy in tx_in:
        copy.wait_recv()
    table_out[...] = (t_x[0] + t_x[1]) + (t_x[2] + t_x[3])

    for copy in gz_in:
        copy.wait_recv()
    piece = g_z[0].astype(F32)
    for k in range(1, 8):
        piece = piece + g_z[k].astype(F32)
    g_oy[y] = piece.astype(BF16)
    oy_in = [remote(g_oy.at[y], g_oy.at[y], S_OY + k - 1, at_y(k)) for k in (1, 2, 3)]
    for copy in oy_in:
        copy.wait_recv()
    oc_in = remote(g_oy, g_oc, S_OC, sibling)
    oc_in.wait_recv()
    first = core == 0
    for k in range(4):
        mine = g_oy[k].astype(F32)
        theirs = g_oc[k].astype(F32)
        grad_out[48 * k : 48 * k + 48, 0:384] = jnp.where(first, mine, theirs)
        grad_out[48 * k : 48 * k + 48, 384:768] = jnp.where(first, theirs, mine)
    for copy in sends:
        copy.wait_send()


def local(features, w_qkv, buckets, cell_ids, bias_table, d_attended):
    seq = lax.axis_index("seq")
    types, levels, _ = bias_table.shape
    type_hit = jnp.arange(types, dtype=jnp.int32) == cell_ids[0]
    table_row = jnp.sum(jnp.where(type_hit[:, None, None], bias_table, 0.0), axis=0)
    tile_at = jnp.arange(TPAD, dtype=jnp.int32)
    padded = jnp.stack(
        [jnp.pad(buckets[0, r], (r, TPAD - BT - r), constant_values=-1) for r in range(2)]
    )
    global_tile = 2 * seq - 8 + tile_at
    in_range = (global_tile >= 0) & (global_tile < 2 * NSEQ)
    onehot = padded[:, :, None] == jnp.arange(levels, dtype=jnp.int32)
    bias = jnp.sum(jnp.where(onehot[:, None], table_row.T[None, :, None, :], 0.0), axis=3)
    valid = (padded >= 0) & in_range[None, :]
    bias = jnp.where(valid[:, None, :], bias, NEG)
    bias_in = jnp.broadcast_to(bias.reshape(4, TPAD, 1), (4, TPAD, 128))
    lane = jnp.arange(128, dtype=jnp.int32)
    head_at = jnp.arange(2, dtype=jnp.int32)
    wanted = head_at[None, :, None] * levels + padded[:, None, :]
    oht = ((wanted[..., None] == lane) & (padded >= 0)[:, None, :, None]).astype(F32)
    oht = oht.reshape(4, TPAD, 128)
    hit = jnp.broadcast_to(type_hit[:, None], (types, 128)).astype(F32)

    vmem = pl.BlockSpec(memory_space=pltpu.VMEM)
    hbm = pl.BlockSpec(memory_space=pl.ANY)
    scratch = [
        pltpu.VMEM((1536, 768), BF16),
        pltpu.VMEM((8, 64, 192), BF16),
        pltpu.VMEM((256, 192), BF16),
        pltpu.VMEM((4, 128, 128), BF16),
        pltpu.VMEM((4, 128, 128), BF16),
        pltpu.VMEM((4, TPAD, 128), F32),
        pltpu.VMEM((2, 64, 256), BF16),
        pltpu.VMEM((2, 64, 128), BF16),
        pltpu.VMEM((128, 128), BF16),
        pltpu.VMEM((18, 128, 256), BF16),
        pltpu.VMEM((NWIN, 128, 128), BF16),
        pltpu.VMEM((NWIN, 128, 128), F32),
        pltpu.VMEM((TPAD, 128), F32),
        pltpu.VMEM((TPAD, 128), F32),
        pltpu.VMEM((4, TPAD, 128), F32),
        pltpu.VMEM((4, TPAD, 128), F32),
        pltpu.VMEM((4, 128, 128), F32),
        pltpu.VMEM((4, 128, 128), BF16),
        pltpu.VMEM((4, 128, 128), BF16),
        pltpu.VMEM((4, TPAD, 128), F32),
        pltpu.VMEM((4, TPAD, 128), F32),
        pltpu.VMEM((18, 128, 256), BF16),
        pltpu.VMEM((18, 128, 256), BF16),
        pltpu.VMEM((4, 2, 128, 256), BF16),
        pltpu.VMEM((4, 128, 128), BF16),
        pltpu.VMEM((256, 768), BF16),
        pltpu.VMEM((2, 2, 192, 384), BF16),
        pltpu.VMEM((2, 192, 384), BF16),
        pltpu.VMEM((2, 192, 384), BF16),
        pltpu.VMEM((4, 2, 48, 384), BF16),
        pltpu.VMEM((2, 48, 384), BF16),
        pltpu.VMEM((8, 48, 384), BF16),
        pltpu.VMEM((4, 48, 384), BF16),
        pltpu.VMEM((4, 48, 384), BF16),
        pltpu.VMEM((2, 32, 128), F32),
        pltpu.VMEM((4, 32, 128), F32),
        pltpu.VMEM((8, 32, 128), F32),
        pltpu.VMEM((4, 32, 128), F32),
        pltpu.SemaphoreType.DMA,
        pltpu.SemaphoreType.DMA((N_SEM,)),
        pltpu.SemaphoreType.DMA((N_SEM,)),
    ]
    att, grad, table = pl.pallas_call(
        kernel,
        out_shape=(
            jax.ShapeDtypeStruct((256, 256), BF16),
            jax.ShapeDtypeStruct((192, 768), F32),
            jax.ShapeDtypeStruct((types, 128), F32),
        ),
        in_specs=[vmem, hbm, vmem, vmem, vmem, vmem],
        out_specs=(vmem, vmem, vmem),
        scratch_shapes=scratch,
        compiler_params=pltpu.CompilerParams(collective_id=0, has_side_effects=True),
    )(features, w_qkv, bias_in, oht, hit, d_attended[0])
    grad_table = table[:, : HEADS * levels].reshape(types, HEADS, levels).transpose(0, 2, 1)
    return (att[None], grad, grad_table)


def solution(mesh):
    in_specs = (
        P("seq", "cell"),
        P(),
        P("cell", "seq", None),
        P("cell"),
        P(),
        P("cell", "seq", None),
    )
    out_specs = (P("cell", "seq", None), P("cell", None), P())
    return jax.shard_map(local, mesh=mesh, in_specs=in_specs, out_specs=out_specs, check_vma=False)
```

time: 761 us -> 104 us (0.14)
  waiting for transfers between devices: 353 us -> 0 us
  blocking collectives: 142 us -> 0 us
  matrix products: 100 us -> 0 us
  Pallas kernels: 0 us -> 91.4 us
  starting transfers between devices: 58.3 us -> 0 us
  local copies, waits for them, and re-layouts: 57.9 us -> 8.88 us
  other arithmetic: 29 us -> 1.87 us
  between operations: 15.1 us -> 1.33 us
    psum x2 -> x0, waiting for transfers between devices: 308 us -> none  [the longest x1 188 us: local(): grad_qkv = lax.psum(share, 'seq')]
    psum x2 -> x0, blocking collectives: 142 us -> none  [the longest x1 79.9 us: local(): grad_table = lax.psum(table_term, ('cell', 'seq'))]
    dot_general x101 -> x0, matrix products: 100 us -> none  [the longest x18 22.1 us: band_scores(): jnp.einsum('qhd,khd->qhk', query_rows, key_rows, preferred_element_type=j...]
    pallas_call x0 -> x1, Pallas kernels: none -> 91.4 us  [local(): pl.pallas_call(kernel, out_shape=(jax.ShapeDtypeStruct((256, 256), BF16),...]
    ppermute x16 -> x0, starting transfers between devices: 58.2 us -> none  [passed_along(): return lax.ppermute(block, axis, route)]
    ppermute x16 -> x0, waiting for transfers between devices: 45 us -> none  [passed_along(): return lax.ppermute(block, axis, route)]
    add x45 -> x3, local copies, waits for them, and re-layouts: 26.1 us -> 0.09 us  [local(): wanted = head_at[None, :, None] * levels + padded[:, None, :]]
    reduce_sum x37 -> x1, other arithmetic: 12.1 us -> 0.09 us  [local(): jnp.sum(jnp.where(onehot[:, None], table_row.T[None, :, None, :], 0.0), a...]
  transfers between devices with their start and end apart: 18 -> 0, of which waited for: 8 -> 0; matrix products, arithmetic and copies ran while one was open for 1% -> 0% of each run, Pallas kernels for 0% -> 0%
where the time goes in v1:
time: 104 us; the launch traced here: 103 us
  Pallas kernels  91.4 us (88%)
  local copies, waits for them, and re-layouts  8.88 us (9%)
  other arithmetic  1.87 us (2%)
  between operations  1.33 us (1%)
    pallas_call x1, Pallas kernels, local(): pl.pallas_call(kernel, out_shape=(jax.ShapeDtypeStruct((256, 256), BF16),...  91.4 us
    unnamed x3, local copies, waits for them, and re-layouts  5.13 us

profile of v1, /device:TPU:1, one launch (start us, length us, event | category | flops | bytes accessed | tf_op | source)
XLA Modules:
  0.0 103.5 jit_solution(265806524321657834)
XLA Ops:
  0.6 0.8 slice_bitcast_fusion.1
  1.4 0.1 pad_bitcast_fusion
  1.5 0.1 iota_compare_fusion.1
  2.2 0.9 select_reduce_fusion.1
  3.1 0.1 select_reduce_fusion
  3.2 0.7 broadcast_in_dim.77.bias_ref
  3.9 0.1 add.41
  4.0 0.1 broadcast_add_fusion
  4.1 0.7 fusion.1.oht_ref
  4.8 0.7 broadcast_in_dim.78.hit_ref
  5.5 1.7 %copy.10.feat_ref = bf16[256,192]{1,0:T(8,128)(2,1)} copy(bf16[256,192]{0,1:T(8,128)(2,1)} %param.6) | data formatting | bytes 196608 | tf_op args[0]
  7.2 91.4 %shard_map.85 = (bf16[256,256]{1,0:T(8,128)(2,1)}, f32[192,768]{1,0:T(8,128)}, f32[32,128]{1,0:T(8,128)}) custom-call(bf16[256,192]{1,0:T(8,128)(2,1)} %copy.10.feat_ref, bf16[1536,768]{1,0:T(8,128)(2,1)} %w_hbm.1, f32[4,24,128]{2,1,0:T(8,128)} %broadcast_in_dim.77.bias_ref, f32[4,24,128]{2,1,0:T(8,128)} %fusion.1.oht_ref, ...), custom_call_target="tpu_custom_call" | custom-call | tf_op jit(solution)/shard_map/pallas_call | solution.py:461
  98.6 1.4 %reshape.102 = f32[32,2,32]{2,1,0:T(2,128)} reshape(f32[32,64]{1,0:T(8,128)} %bitcast.20) | data formatting | bytes 16384 | tf_op jit(solution)/shard_map/reshape | solution.py:473
  100.0 1.6 %copy.14 = bf16[1,256,256]{2,1,0:T(8,128)(2,1)} copy(bf16[1,256,256]{2,1,0:T(8,128)(2,1)} %bitcast.17) | data formatting | bytes 262144
  101.5 1.9 %copy.15 = f32[192,768]{1,0:T(8,128)} copy(f32[192,768]{1,0:T(8,128)} %get-tuple-element.21) | data formatting | bytes 1179648
  (10 shorter events, 0.1 us)

commit v2 on v1

--- a/solution.py
+++ b/solution.py
@@ -25,7 +25,8 @@
 S_BIAS = 11
 S_KV = 14
 S_Q = 17
-S_WIN = 18
+S_NEAR = 18
+S_FAR = 22
 S_ATT = 26
 S_TT = 29
 S_DKV = 32
@@ -40,7 +41,9 @@
 S_TX = 68
 S_OY = 71
 S_OC = 74
-N_SEM = 75
+S_SIB = 75
+S_GC2 = 83
+N_SEM = 84
 
 WIN_OFFSETS = (-4, 4, -3, 3, -2, 2, -1, 1)
 
@@ -58,13 +61,13 @@
 
 
 def kernel(
-    feat_ref, w_hbm, bias_ref, oht_ref, hit_ref, dout_ref,
+    ft_hbm, w_hbm, buckets_ref, ids_ref, tbl_hbm, dout_hbm,
     att_out, grad_out, table_out,
-    w_ref, fbuf, fcross, dot_src, dot_buf, bias_buf, proj_kv, proj_q, q_buf, kvw,
+    ft_ref, feat_ref, dout_ref, tbl_ref, row_buf, oh_buf, bias_ref, w_ref, fbuf, fcross, dot_src, dot_buf, bias_buf, proj_kv, proj_q, q_buf, kvw,
     e0_buf, o_buf, m_buf, l_buf, d_buf, w_buf, dof_buf,
     att_src, att_buf, tt_src, tt_buf, dkvw, dkv_in, dkv_x, dq_x, d3,
-    g_src, g_core, g_c, g_y, g_zs, g_z, g_oy, g_oc,
-    t_c, t_y, t_z, t_x, w_sem, send_sem, recv_sem,
+    g_src, g_mine, g_core, g_c, g_y, g_zs, g_z, g_oy, g_oc,
+    t_c, t_y, t_z, t_x, in_sem, send_sem, recv_sem,
 ):
     cell = lax.axis_index("cell")
     seq = lax.axis_index("seq")
@@ -95,12 +98,11 @@
 
     sibling = (cell, seq + 1 - 2 * core)
 
-    w_copy = pltpu.make_async_copy(w_hbm, w_ref, w_sem)
-    w_copy.start()
-
+    ft_copy = pltpu.make_async_copy(ft_hbm, ft_ref, in_sem.at[0])
+    ft_copy.start()
     barrier = pltpu.get_barrier_semaphore()
     greet = [at_cross(k) for k in range(4)] + [at_x(k) for k in (1, 2, 3)]
-    greet += [at_seq(o) for o in WIN_OFFSETS]
+    greet += [at_seq(o) for o in WIN_OFFSETS] + [sibling]
     greet += [at_y(k) for k in (1, 2, 3)] + [at_z(k) for k in range(1, 8)]
     for peer in greet:
         pl.semaphore_signal(barrier, inc=1, device_id=peer, device_id_type=pl.DeviceIdType.MESH)
@@ -120,11 +122,14 @@
         sends.append(copy)
         return copy
 
-    for piece in range(4):
-        r, h = piece // 2, piece % 2
-        block = dout_ref[128 * r : 128 * r + 128, 128 * h : 128 * h + 128]
-        dot_src[piece] = block.astype(F32).T.astype(BF16)
-
+    dout_copy = pltpu.make_async_copy(dout_hbm.at[0], dout_ref, in_sem.at[1])
+    dout_copy.start()
+    tbl_copy = pltpu.make_async_copy(tbl_hbm, tbl_ref, in_sem.at[2])
+    tbl_copy.start()
+    w_copy = pltpu.make_async_copy(w_hbm, w_ref, in_sem.at[3])
+    w_copy.start()
+    ft_copy.wait()
+    feat_ref[...] = ft_ref[...].astype(F32).T.astype(BF16)
     pl.semaphore_wait(barrier, len(greet))
 
     feat_in = []
@@ -138,13 +143,38 @@
         feat_in.append(
             remote(feat_ref.at[pl.ds(64 * there, 64)], fbuf.at[cell], S_FEAT + 3 + k, at_x(k))
         )
+    dout_copy.wait()
+    for piece in range(4):
+        r, h = piece // 2, piece % 2
+        block = dout_ref[128 * r : 128 * r + 128, 128 * h : 128 * h + 128]
+        dot_src[piece] = block.astype(F32).T.astype(BF16)
+    lane = lax.broadcasted_iota(jnp.int32, (1, 128), 1)
+    oh_buf[...] = jnp.zeros((2, TPAD, 128), F32)
+    row_buf[...] = jnp.zeros((8, 128), F32)
+    for r in range(2):
+        for o in range(BT):
+            oh_buf[r, r + o : r + o + 1, :] = (lane == buckets_ref[0, r, o]).astype(F32)
+    tbl_copy.wait()
+    hit = (lax.broadcasted_iota(jnp.int32, (32, 128), 0) == ids_ref[0]).astype(F32)
+    tile_at = lax.broadcasted_iota(jnp.int32, (TPAD, 128), 0)
+    global_tile = 2 * seq - 8 + tile_at
+    in_range = (global_tile >= 0) & (global_tile < 2 * NSEQ)
+    for h in range(2):
+        row_buf[h : h + 1, 0:32] = jnp.sum(
+            jnp.where(hit[:, 0:32] > 0.0, tbl_ref[:, h, :], 0.0), axis=0, keepdims=True
+        )
+        for r in range(2):
+            level = jnp.sum(oh_buf[r] * row_buf[h : h + 1, :], axis=1, keepdims=True)
+            valid = in_range & (tile_at >= r) & (tile_at < r + BT)
+            bias_ref[2 * r + h] = jnp.where(valid, jnp.broadcast_to(level, (TPAD, 128)), NEG)
+
     do_in = []
     bias_in = []
     for k in (1, 2, 3):
         there = (x + k) % 4
         do_in.append(remote(dot_src.at[there], dot_buf.at[x], S_DO + k - 1, at_x(k)))
         bias_in.append(remote(bias_ref.at[there], bias_buf.at[x], S_BIAS + k - 1, at_x(k)))
-    cross_in = remote(feat_ref, fcross, S_FCROSS, at_cross(0))
+    cross_in = remote(ft_ref, fcross, S_FCROSS, at_cross(0))
 
     dot_buf[x] = dot_src[x]
     bias_buf[x] = bias_ref[x]
@@ -177,12 +207,33 @@
     for copy in kv_in:
         copy.wait_recv()
 
-    win_in = {}
-    for n, o in enumerate(WIN_OFFSETS):
-        count = 1 if o == -4 else 2
-        win_in[4 - o] = remote(
-            kvw.at[pl.ds(8, count)], kvw.at[pl.ds(8 - 2 * o, count)], S_WIN + n, at_seq(o)
-        )
+    def relay(src_tile, dst_tile, slot):
+        return remote(kvw.at[src_tile], kvw.at[dst_tile], slot, sibling)
+
+    near = {}
+    far = {}
+    mate_in = {}
+    pairs = [(t, d) for t in range(2) for d in (-1, 1)]
+    for n, (t, d) in enumerate(pairs):
+        near[-d, t] = remote(kvw.at[8 + t], kvw.at[8 - 4 * d + t], S_NEAR + n, at_seq(2 * d))
+    for t in range(2):
+        mate_in[0, t] = relay(8 + t, 6 + 4 * core + t, S_SIB + t)
+
+    def pass_on(t):
+        for d in (-1, 1):
+            near[d, t].wait_recv()
+            here = 8 + 4 * d + t
+            n = pairs.index((t, d))
+            far[2 * d, t] = remote(
+                kvw.at[here], kvw.at[8 + 8 * d + t], S_FAR + n, at_seq(-2 * d)
+            )
+            mate_in[d, t] = relay(here, 6 + 4 * d + 4 * core + t, S_SIB + 2 + n)
+
+    def pass_far(t):
+        for d in (-2, 2):
+            far[d, t].wait_recv()
+        mate_in[2, t] = relay(16 - 16 * core + t, 14 - 12 * core + t, S_SIB + 6 + t)
+
     q_in.wait_recv()
     for copy in do_in + bias_in:
         copy.wait_recv()
@@ -200,21 +251,37 @@
         s = dot_nt(keys, q_tile) * FACTOR
         top = jnp.max(s, axis=0, keepdims=True)
         e0 = jnp.exp(s - top)
-        m_buf[t : t + 1, :] = top
-        l_buf[t : t + 1, :] = jnp.sum(e0, axis=0, keepdims=True)
+        m_buf[pl.ds(t, 1), :] = top
+        l_buf[pl.ds(t, 1), :] = jnp.sum(e0, axis=0, keepdims=True)
         e0b = e0.astype(BF16)
         e0_buf[t] = e0b
         o_t = dot_tn(values, e0b)
         o_buf[t] = o_t
         for c in range(4):
-            d_buf[c, t : t + 1, :] = jnp.sum(dof_buf[c] * o_t, axis=0, keepdims=True)
-
-    for slot in (4, 3, 5, 2, 6, 1, 7, 0, 8):
-        if slot != 4:
-            win_in[slot].wait_recv()
-        forward_tile(2 * slot)
-        if slot != 8:
-            forward_tile(2 * slot + 1)
+            d_buf[c, pl.ds(t, 1), :] = jnp.sum(dof_buf[c] * o_t, axis=0, keepdims=True)
+
+    forward_tile(8)
+    pass_on(0)
+    forward_tile(9)
+    pass_on(1)
+    for t in range(2):
+        mate_in[0, t].wait_recv()
+        forward_tile(10 - 4 * core + t)
+    for t in range(2):
+        for d in (-1, 1):
+            forward_tile(8 + 4 * d + t)
+    pass_far(0)
+    for t in range(2):
+        for d in (-1, 1):
+            mate_in[d, t].wait_recv()
+            forward_tile(10 + 4 * d - 4 * core + t)
+    pass_far(1)
+    forward_tile(0)
+    forward_tile(1)
+    forward_tile(16)
+    for t in range(2):
+        mate_in[2, t].wait_recv()
+        forward_tile(2 + 12 * core + t)
 
     m_all = m_buf[...]
     l_all = l_buf[...]
@@ -275,17 +342,21 @@
     for copy in tt_in:
         copy.wait_recv()
     ones = jnp.ones((8, 128), F32)
-    row = jnp.zeros((8, 128), F32)
-    for piece in range(4):
-        sums = lax.dot_general(
-            ones, tt_buf[piece], (((1,), (1,)), ((), ())),
-            precision=lax.Precision.HIGHEST, preferred_element_type=F32,
-        )
-        row = row + lax.dot_general(
-            sums, oht_ref[piece], (((1,), (0,)), ((), ())),
-            precision=lax.Precision.HIGHEST, preferred_element_type=F32,
-        )
-    t_c[core] = hit_ref[...] * row[0:1, :]
+    rows = []
+    for h in range(2):
+        row = jnp.zeros((8, 128), F32)
+        for r in range(2):
+            sums = lax.dot_general(
+                ones, tt_buf[2 * r + h], (((1,), (1,)), ((), ())),
+                precision=lax.Precision.HIGHEST, preferred_element_type=F32,
+            )
+            row = row + lax.dot_general(
+                sums, oh_buf[r], (((1,), (0,)), ((), ())),
+                precision=lax.Precision.HIGHEST, preferred_element_type=F32,
+            )
+        rows.append(row)
+    both_heads = rows[0] + pltpu.roll(rows[1], 32, axis=1)
+    t_c[core] = hit * both_heads[0:1, :]
     tc_in = remote(t_c.at[core], t_c.at[core], S_TC, sibling)
 
     for copy in att_in:
@@ -313,30 +384,32 @@
     for copy in xq_in + xkv_in:
         copy.wait_recv()
     for t in range(2):
+        at_rows = slice(128 * t, 128 * t + 128)
         for h in range(2):
-            rows = slice(128 * t, 128 * t + 128)
-            d3[rows, 128 * h : 128 * h + 128] = dq_x[2 * t + h]
+            d3[0, at_rows, 128 * h : 128 * h + 128] = dq_x[2 * t + h]
             both = dkv_x[h, t].astype(F32) + dkv_x[2 + h, t].astype(F32)
             bothb = both.astype(BF16)
-            d3[rows, 256 + 128 * h : 384 + 128 * h] = bothb[:, 0:128]
-            d3[rows, 512 + 128 * h : 640 + 128 * h] = bothb[:, 128:256]
+            d3[h, at_rows, 256 - 256 * h : 384 - 256 * h] = bothb[:, 0:128]
+            d3[1, at_rows, 128 + 128 * h : 256 + 128 * h] = bothb[:, 128:256]
 
     cross_in.wait_recv()
-    d_all = d3[...]
-    own = dot_tn(feat_ref[...], d_all).astype(BF16)
-    other = dot_tn(fcross[...], d_all).astype(BF16)
-    for k in range(2):
-        g_src[k, zh] = own[:, 384 * k : 384 * k + 384]
-        g_src[k, 1 - zh] = other[:, 384 * k : 384 * k + 384]
-    gc_in = remote(g_src.at[1 - core], g_core, S_GC, sibling)
+    theirs = d3[1 - core]
+    g_src[zh] = dot_nn(ft_ref[...], theirs).astype(BF16)
+    gc_in = [remote(g_src.at[zh], g_core.at[zh], S_GC, sibling)]
+    g_src[1 - zh] = dot_nn(fcross[...], theirs).astype(BF16)
+    gc_in.append(remote(g_src.at[1 - zh], g_core.at[1 - zh], S_GC2, sibling))
+    mine = d3[core]
+    g_mine[zh] = dot_nn(ft_ref[...], mine)
+    g_mine[1 - zh] = dot_nn(fcross[...], mine)
 
     for copy in ty_in:
         copy.wait_recv()
     t_z[zi] = (t_y[0] + t_y[1]) + (t_y[2] + t_y[3])
     tz_in = [remote(t_z.at[zi], t_z.at[zi], S_TZ + k - 1, at_z(k)) for k in range(1, 8)]
 
-    gc_in.wait_recv()
-    g_c[...] = (g_src[core].astype(F32) + g_core[...].astype(F32)).astype(BF16)
+    for copy in gc_in:
+        copy.wait_recv()
+    g_c[...] = (g_mine[...] + g_core[...].astype(F32)).astype(BF16)
     gy_in = []
     for k in (1, 2, 3):
         there = (y + k) % 4
@@ -380,45 +453,37 @@
         copy.wait_recv()
     oc_in = remote(g_oy, g_oc, S_OC, sibling)
     oc_in.wait_recv()
-    first = core == 0
-    for k in range(4):
-        mine = g_oy[k].astype(F32)
-        theirs = g_oc[k].astype(F32)
-        grad_out[48 * k : 48 * k + 48, 0:384] = jnp.where(first, mine, theirs)
-        grad_out[48 * k : 48 * k + 48, 384:768] = jnp.where(first, theirs, mine)
+    grad_out[core] = g_oy[...]
+    grad_out[1 - core] = g_oc[...]
     for copy in sends:
         copy.wait_send()
 
 
+def finish(att_ref, pieces_ref, table_ref, att_out, grad_out, table_out):
+    att_out[0] = att_ref[...]
+    for k in range(2):
+        for n in range(4):
+            grad_out[48 * n : 48 * n + 48, 384 * k : 384 * k + 384] = pieces_ref[k, n].astype(F32)
+    for h in range(2):
+        table_out[:, h, :] = table_ref[:, 32 * h : 32 * h + 32]
+
+
 def local(features, w_qkv, buckets, cell_ids, bias_table, d_attended):
-    seq = lax.axis_index("seq")
     types, levels, _ = bias_table.shape
-    type_hit = jnp.arange(types, dtype=jnp.int32) == cell_ids[0]
-    table_row = jnp.sum(jnp.where(type_hit[:, None, None], bias_table, 0.0), axis=0)
-    tile_at = jnp.arange(TPAD, dtype=jnp.int32)
-    padded = jnp.stack(
-        [jnp.pad(buckets[0, r], (r, TPAD - BT - r), constant_values=-1) for r in range(2)]
-    )
-    global_tile = 2 * seq - 8 + tile_at
-    in_range = (global_tile >= 0) & (global_tile < 2 * NSEQ)
-    onehot = padded[:, :, None] == jnp.arange(levels, dtype=jnp.int32)
-    bias = jnp.sum(jnp.where(onehot[:, None], table_row.T[None, :, None, :], 0.0), axis=3)
-    valid = (padded >= 0) & in_range[None, :]
-    bias = jnp.where(valid[:, None, :], bias, NEG)
-    bias_in = jnp.broadcast_to(bias.reshape(4, TPAD, 1), (4, TPAD, 128))
-    lane = jnp.arange(128, dtype=jnp.int32)
-    head_at = jnp.arange(2, dtype=jnp.int32)
-    wanted = head_at[None, :, None] * levels + padded[:, None, :]
-    oht = ((wanted[..., None] == lane) & (padded >= 0)[:, None, :, None]).astype(F32)
-    oht = oht.reshape(4, TPAD, 128)
-    hit = jnp.broadcast_to(type_hit[:, None], (types, 128)).astype(F32)
-
     vmem = pl.BlockSpec(memory_space=pltpu.VMEM)
     hbm = pl.BlockSpec(memory_space=pl.ANY)
+    smem = pl.BlockSpec(memory_space=pltpu.SMEM)
     scratch = [
+        pltpu.VMEM((192, 256), BF16),
+        pltpu.VMEM((256, 192), BF16),
+        pltpu.VMEM((256, 256), BF16),
+        pltpu.VMEM((32, 2, 32), F32),
+        pltpu.VMEM((8, 128), F32),
+        pltpu.VMEM((2, TPAD, 128), F32),
+        pltpu.VMEM((4, TPAD, 128), F32),
         pltpu.VMEM((1536, 768), BF16),
         pltpu.VMEM((8, 64, 192), BF16),
-        pltpu.VMEM((256, 192), BF16),
+        pltpu.VMEM((192, 256), BF16),
         pltpu.VMEM((4, 128, 128), BF16),
         pltpu.VMEM((4, 128, 128), BF16),
         pltpu.VMEM((4, TPAD, 128), F32),
@@ -441,8 +506,9 @@
         pltpu.VMEM((18, 128, 256), BF16),
         pltpu.VMEM((4, 2, 128, 256), BF16),
         pltpu.VMEM((4, 128, 128), BF16),
-        pltpu.VMEM((256, 768), BF16),
-        pltpu.VMEM((2, 2, 192, 384), BF16),
+        pltpu.VMEM((2, 256, 384), BF16),
+        pltpu.VMEM((2, 192, 384), BF16),
+        pltpu.VMEM((2, 192, 384), F32),
         pltpu.VMEM((2, 192, 384), BF16),
         pltpu.VMEM((2, 192, 384), BF16),
         pltpu.VMEM((4, 2, 48, 384), BF16),
@@ -454,7 +520,7 @@
         pltpu.VMEM((4, 32, 128), F32),
         pltpu.VMEM((8, 32, 128), F32),
         pltpu.VMEM((4, 32, 128), F32),
-        pltpu.SemaphoreType.DMA,
+        pltpu.SemaphoreType.DMA((4,)),
         pltpu.SemaphoreType.DMA((N_SEM,)),
         pltpu.SemaphoreType.DMA((N_SEM,)),
     ]
@@ -462,16 +528,25 @@
         kernel,
         out_shape=(
             jax.ShapeDtypeStruct((256, 256), BF16),
-            jax.ShapeDtypeStruct((192, 768), F32),
+            jax.ShapeDtypeStruct((2, 4, 48, 384), BF16),
             jax.ShapeDtypeStruct((types, 128), F32),
         ),
-        in_specs=[vmem, hbm, vmem, vmem, vmem, vmem],
+        in_specs=[hbm, hbm, smem, smem, hbm, hbm],
         out_specs=(vmem, vmem, vmem),
         scratch_shapes=scratch,
         compiler_params=pltpu.CompilerParams(collective_id=0, has_side_effects=True),
-    )(features, w_qkv, bias_in, oht, hit, d_attended[0])
-    grad_table = table[:, : HEADS * levels].reshape(types, HEADS, levels).transpose(0, 2, 1)
-    return (att[None], grad, grad_table)
+    )(features.T, w_qkv, buckets, cell_ids, bias_table.transpose(0, 2, 1), d_attended)
+    att, grad, table = pl.pallas_call(
+        finish,
+        out_shape=(
+            jax.ShapeDtypeStruct((1, 256, 256), BF16),
+            jax.ShapeDtypeStruct((192, 768), F32),
+            jax.ShapeDtypeStruct((types, HEADS, levels), F32),
+        ),
+        in_specs=[vmem] * 3,
+        out_specs=(vmem,) * 3,
+    )(att, grad, table)
+    return (att, grad, table.transpose(0, 2, 1))
 
 
 def solution(mesh):

time: 104 us -> 91.6 us (0.88)
  local copies, waits for them, and re-layouts: 8.88 us -> 0 us
  other arithmetic: 1.87 us -> 0 us
  Pallas kernels: 91.4 us -> 90.2 us
    unnamed x3 -> x0, local copies, waits for them, and re-layouts: 5.13 us -> none
    pallas_call x1, Pallas kernels: 91.4 us -> 88.2 us  [local(): pl.pallas_call(kernel, out_shape=(jax.ShapeDtypeStruct((256, 256), BF16),...]
    pallas_call x0 -> x1, Pallas kernels: none -> 1.92 us  [local(): pl.pallas_call(finish, out_shape=(jax.ShapeDtypeStruct((1, 256, 256), BF1...]
    reshape x1 -> x0, local copies, waits for them, and re-layouts: 1.42 us -> none  [local(): table[:, :HEADS * levels].reshape(types, HEADS, levels).transpose(0, 2, 1)]
    broadcast_in_dim x2 -> x0, local copies, waits for them, and re-layouts: 1.37 us -> none  [the longest x1 0.7 us: local(): bias_in = jnp.broadcast_to(bias.reshape(4, TPAD, 1), (4, TPAD, 128))]
where the time goes in v2:
time: 91.6 us; the launch traced here: 91.4 us
  Pallas kernels  90.2 us (98%)
  between operations  1.29 us (1%)
    pallas_call x1, Pallas kernels, local(): pl.pallas_call(kernel, out_shape=(jax.ShapeDtypeStruct((256, 256), BF16),...  88.2 us
    pallas_call x1, Pallas kernels, local(): pl.pallas_call(finish, out_shape=(jax.ShapeDtypeStruct((1, 256, 256), BF1...  1.92 us

profile of v2, /device:TPU:1, one launch (start us, length us, event | category | flops | bytes accessed | tf_op | source)
XLA Modules:
  0.0 91.4 jit_solution(4911430136202210195)
XLA Ops:
  1.3 88.2 %shard_map.85 = (bf16[256,256]{1,0:T(8,128)(2,1)}, bf16[2,4,48,384]{3,2,1,0:T(8,128)(2,1)}, f32[32,128]{1,0:T(8,128)}) custom-call(bf16[192,256]{1,0:T(8,128)(2,1)} %bitcast.3, bf16[1536,768]{1,0:T(8,128)(2,1)} %w_hbm.1, s32[1,2,16]{2,1,0:T(2,128)} %buckets_ref.1, s32[1]{0:T(128)S(6)} %copy.9.ids_ref, f32[32,2,32]{2,1,0:T(2,128)} %bitcast.4, ...), custom_call_target="tpu_custom_call" | custom-call | tf_op jit(solution)/shard_map/pallas_call | solution.py:527
  89.5 1.9 %shard_map.86 = (bf16[1,256,256]{2,1,0:T(8,128)(2,1)}, f32[192,768]{1,0:T(8,128)}, f32[32,2,32]{2,1,0:T(2,128)}) custom-call(bf16[256,256]{1,0:T(8,128)(2,1)} %get-tuple-element.9.att_ref, bf16[2,4,48,384]{3,2,1,0:T(8,128)(2,1)} %get-tuple-element.10.pieces_ref, f32[32,128]{1,0:T(8,128)} %get-tuple-element.11.table_ref), custom_call_target="tpu_custom_call" | custom-call | tf_op jit(solution)/shard_map/pallas_call | solution.py:539

commit v3 on v2

--- a/solution.py
+++ b/solution.py
@@ -60,6 +60,29 @@
     return lax.dot_general(a, b, (((0,), (0,)), ((), ())), preferred_element_type=F32)
 
 
+class Copy:
+    def __init__(self, copy, sends, receives):
+        self.copy = copy
+        self.sends = sends
+        self.receives = receives
+        if sends is None:
+            copy.start()
+        else:
+            pl.when(sends)(copy.start)
+
+    def wait_recv(self):
+        if self.receives is None:
+            self.copy.wait_recv()
+        else:
+            pl.when(self.receives)(self.copy.wait_recv)
+
+    def wait_send(self):
+        if self.sends is None:
+            self.copy.wait_send()
+        else:
+            pl.when(self.sends)(self.copy.wait_send)
+
+
 def kernel(
     ft_hbm, w_hbm, buckets_ref, ids_ref, tbl_hbm, dout_hbm,
     att_out, grad_out, table_out,
@@ -102,14 +125,31 @@
     ft_copy.start()
     barrier = pltpu.get_barrier_semaphore()
     greet = [at_cross(k) for k in range(4)] + [at_x(k) for k in (1, 2, 3)]
-    greet += [at_seq(o) for o in WIN_OFFSETS] + [sibling]
+    greet += [sibling]
     greet += [at_y(k) for k in (1, 2, 3)] + [at_z(k) for k in range(1, 8)]
     for peer in greet:
         pl.semaphore_signal(barrier, inc=1, device_id=peer, device_id_type=pl.DeviceIdType.MESH)
+    chip = seq // 2
+
+    def chip_in(d):
+        return (chip + d >= 0) & (chip + d < NSEQ // 2)
+
+    def seq_in(o):
+        return (seq + o >= 0) & (seq + o < NSEQ)
+
+    expected = len(greet)
+    for o in WIN_OFFSETS:
+        @pl.when(seq_in(o))
+        def _():
+            pl.semaphore_signal(
+                barrier, inc=1, device_id=at_seq(o), device_id_type=pl.DeviceIdType.MESH
+            )
+
+        expected = expected + seq_in(o).astype(jnp.int32)
 
     sends = []
 
-    def remote(src, dst, slot, peer):
+    def remote(src, dst, slot, peer, if_send=None, if_recv=None):
         copy = pltpu.make_async_remote_copy(
             src_ref=src,
             dst_ref=dst,
@@ -118,7 +158,7 @@
             device_id=peer,
             device_id_type=pl.DeviceIdType.MESH,
         )
-        copy.start()
+        copy = Copy(copy, if_send, if_recv)
         sends.append(copy)
         return copy
 
@@ -129,20 +169,21 @@
     w_copy = pltpu.make_async_copy(w_hbm, w_ref, in_sem.at[3])
     w_copy.start()
     ft_copy.wait()
-    feat_ref[...] = ft_ref[...].astype(F32).T.astype(BF16)
-    pl.semaphore_wait(barrier, len(greet))
-
-    feat_in = []
-    for k in range(4):
+    feat = ft_ref[...].astype(F32).T.astype(BF16)
+    for n in range(4):
+        rows = feat[64 * n : 64 * n + 64]
+        feat_ref[n, 0:64, :] = rows[:, 0:128]
+        feat_ref[n, 64:96, 0:64] = rows[0:32, 128:192]
+        feat_ref[n, 64:96, 64:128] = rows[32:64, 128:192]
+    pl.semaphore_wait(barrier, expected)
+
+    feat_in = {}
+    for k in (2, 1, 3, 0):
         there = (x + k) % 4
-        feat_in.append(
-            remote(feat_ref.at[pl.ds(64 * there, 64)], fbuf.at[cell], S_FEAT + k, at_cross(k))
-        )
-    for k in (1, 2, 3):
+        feat_in[1, k] = remote(feat_ref.at[there], fbuf.at[cell], S_FEAT + k, at_cross(k))
+    for k in (1, 3, 2):
         there = (x + k) % 4
-        feat_in.append(
-            remote(feat_ref.at[pl.ds(64 * there, 64)], fbuf.at[cell], S_FEAT + 3 + k, at_x(k))
-        )
+        feat_in[0, k] = remote(feat_ref.at[there], fbuf.at[cell], S_FEAT + 3 + k, at_x(k))
     dout_copy.wait()
     for piece in range(4):
         r, h = piece // 2, piece % 2
@@ -178,14 +219,30 @@
 
     dot_buf[x] = dot_src[x]
     bias_buf[x] = bias_ref[x]
-    fbuf[cell] = feat_ref[pl.ds(64 * x, 64), :]
+    fbuf[cell] = feat_ref[x]
+    for t in range(18):
+        tile = 2 * seq - 8 + t
+
+        @pl.when((tile < 0) | (tile >= 2 * NSEQ))
+        def _():
+            kvw[t] = jnp.zeros((128, 256), BF16)
+            dkv_in[t] = jnp.zeros((128, 256), BF16)
+
     w_copy.wait()
-    for copy in feat_in:
-        copy.wait_recv()
-
-    proj = jnp.zeros((64, 768), F32)
-    for c in range(8):
-        proj = proj + dot_nn(fbuf[c], w_ref[192 * c : 192 * c + 192, :])
+
+    def project(c):
+        rows = fbuf[c]
+        low = pl.multiple_of(192 * c, 64)
+        tail = jnp.concatenate([rows[64:96, 0:64], rows[64:96, 64:128]], axis=0)
+        return dot_nn(rows[0:64], w_ref[pl.ds(low, 128), :]) + dot_nn(
+            tail, w_ref[pl.ds(pl.multiple_of(low + 128, 64), 64), :]
+        )
+
+    proj = project(cell)
+    for z, k in ((0, 1), (0, 3), (0, 2), (1, 2), (1, 1), (1, 3), (1, 0)):
+        feat_in[z, k].wait_recv()
+        half_from = zh if z == 0 else 1 - zh
+        proj = proj + project(half_from * 4 + (x - k + 4) % 4)
     projected = proj.astype(BF16)
     for h in range(2):
         proj_q[h] = projected[:, 128 * h : 128 * h + 128]
@@ -207,15 +264,24 @@
     for copy in kv_in:
         copy.wait_recv()
 
-    def relay(src_tile, dst_tile, slot):
-        return remote(kvw.at[src_tile], kvw.at[dst_tile], slot, sibling)
+    def relay(src_tile, dst_tile, slot, if_send=None, if_recv=None):
+        return remote(
+            kvw.at[src_tile], kvw.at[dst_tile], slot, sibling, if_send, if_recv
+        )
 
     near = {}
     far = {}
     mate_in = {}
     pairs = [(t, d) for t in range(2) for d in (-1, 1)]
     for n, (t, d) in enumerate(pairs):
-        near[-d, t] = remote(kvw.at[8 + t], kvw.at[8 - 4 * d + t], S_NEAR + n, at_seq(2 * d))
+        near[-d, t] = remote(
+            kvw.at[8 + t],
+            kvw.at[8 - 4 * d + t],
+            S_NEAR + n,
+            at_seq(2 * d),
+            chip_in(d),
+            chip_in(-d),
+        )
     for t in range(2):
         mate_in[0, t] = relay(8 + t, 6 + 4 * core + t, S_SIB + t)
 
@@ -225,14 +291,27 @@
             here = 8 + 4 * d + t
             n = pairs.index((t, d))
             far[2 * d, t] = remote(
-                kvw.at[here], kvw.at[8 + 8 * d + t], S_FAR + n, at_seq(-2 * d)
+                kvw.at[here],
+                kvw.at[8 + 8 * d + t],
+                S_FAR + n,
+                at_seq(-2 * d),
+                chip_in(d) & chip_in(-d),
+                chip_in(2 * d),
             )
-            mate_in[d, t] = relay(here, 6 + 4 * d + 4 * core + t, S_SIB + 2 + n)
+            mate_in[d, t] = relay(
+                here, 6 + 4 * d + 4 * core + t, S_SIB + 2 + n, chip_in(d), chip_in(d)
+            )
 
     def pass_far(t):
         for d in (-2, 2):
             far[d, t].wait_recv()
-        mate_in[2, t] = relay(16 - 16 * core + t, 14 - 12 * core + t, S_SIB + 6 + t)
+        mate_in[2, t] = relay(
+            16 - 16 * core + t,
+            14 - 12 * core + t,
+            S_SIB + 6 + t,
+            chip_in(2 - 4 * core),
+            chip_in(4 * core - 2),
+        )
 
     q_in.wait_recv()
     for copy in do_in + bias_in:
@@ -335,6 +414,8 @@
                 dkv_in.at[pl.ds(2 * (4 - o), count)],
                 S_DKV + n,
                 at_seq(o),
+                seq_in(o),
+                seq_in(-o),
             )
     dq_x[x] = (dq_acc * FACTOR).astype(BF16)
     xq_in = [remote(dq_x.at[x], dq_x.at[x], S_XQ + k - 1, at_x(k)) for k in (1, 2, 3)]
@@ -475,14 +556,14 @@
     smem = pl.BlockSpec(memory_space=pltpu.SMEM)
     scratch = [
         pltpu.VMEM((192, 256), BF16),
-        pltpu.VMEM((256, 192), BF16),
+        pltpu.VMEM((4, 96, 128), BF16),
         pltpu.VMEM((256, 256), BF16),
         pltpu.VMEM((32, 2, 32), F32),
         pltpu.VMEM((8, 128), F32),
         pltpu.VMEM((2, TPAD, 128), F32),
         pltpu.VMEM((4, TPAD, 128), F32),
         pltpu.VMEM((1536, 768), BF16),
-        pltpu.VMEM((8, 64, 192), BF16),
+        pltpu.VMEM((8, 96, 128), BF16),
         pltpu.VMEM((192, 256), BF16),
         pltpu.VMEM((4, 128, 128), BF16),
         pltpu.VMEM((4, 128, 128), BF16),

time: 91.6 us -> 88.6 us (0.967)
  Pallas kernels: 90.2 us -> 87.2 us
    pallas_call x1, Pallas kernels: 88.2 us -> 85.3 us  [local(): pl.pallas_call(kernel, out_shape=(jax.ShapeDtypeStruct((256, 256), BF16),...]
where the time goes in v3:
time: 88.6 us; the launch traced here: 88.5 us
  Pallas kernels  87.2 us (98%)
  between operations  1.29 us (1%)
    pallas_call x1, Pallas kernels, local(): pl.pallas_call(kernel, out_shape=(jax.ShapeDtypeStruct((256, 256), BF16),...  85.3 us
    pallas_call x1, Pallas kernels, local(): pl.pallas_call(finish, out_shape=(jax.ShapeDtypeStruct((1, 256, 256), BF1...  1.92 us

profile of v3, /device:TPU:1, one launch (start us, length us, event | category | flops | bytes accessed | tf_op | source)
XLA Modules:
  0.0 88.5 jit_solution(6193232415282266347)
XLA Ops:
  1.3 85.3 %shard_map.85 = (bf16[256,256]{1,0:T(8,128)(2,1)}, bf16[2,4,48,384]{3,2,1,0:T(8,128)(2,1)}, f32[32,128]{1,0:T(8,128)}) custom-call(bf16[192,256]{1,0:T(8,128)(2,1)} %bitcast.3, bf16[1536,768]{1,0:T(8,128)(2,1)} %w_hbm.1, s32[1,2,16]{2,1,0:T(2,128)} %buckets_ref.1, s32[1]{0:T(128)S(6)} %copy.9.ids_ref, f32[32,2,32]{2,1,0:T(2,128)} %bitcast.4, ...), custom_call_target="tpu_custom_call" | custom-call | tf_op jit(solution)/shard_map/pallas_call | solution.py:608
  86.6 1.9 %shard_map.86 = (bf16[1,256,256]{2,1,0:T(8,128)(2,1)}, f32[192,768]{1,0:T(8,128)}, f32[32,2,32]{2,1,0:T(2,128)}) custom-call(bf16[256,256]{1,0:T(8,128)(2,1)} %get-tuple-element.9.att_ref, bf16[2,4,48,384]{3,2,1,0:T(8,128)(2,1)} %get-tuple-element.10.pieces_ref, f32[32,128]{1,0:T(8,128)} %get-tuple-element.11.table_ref), custom_call_target="tpu_custom_call" | custom-call | tf_op jit(solution)/shard_map/pallas_call | solution.py:620

commit v4 on v3

--- a/solution.py
+++ b/solution.py
@@ -43,9 +43,12 @@
 S_OC = 74
 S_SIB = 75
 S_GC2 = 83
-N_SEM = 84
-
-WIN_OFFSETS = (-4, 4, -3, 3, -2, 2, -1, 1)
+S_XKV2 = 84
+S_DNEAR = 87
+S_DFAR = 91
+N_SEM = 95
+
+CHIP_STEPS = (-2, 2)
 
 
 def dot_nn(a, b):
@@ -88,7 +91,7 @@
     att_out, grad_out, table_out,
     ft_ref, feat_ref, dout_ref, tbl_ref, row_buf, oh_buf, bias_ref, w_ref, fbuf, fcross, dot_src, dot_buf, bias_buf, proj_kv, proj_q, q_buf, kvw,
     e0_buf, o_buf, m_buf, l_buf, d_buf, w_buf, dof_buf,
-    att_src, att_buf, tt_src, tt_buf, dkvw, dkv_in, dkv_x, dq_x, d3,
+    att_src, att_buf, tt_src, tt_buf, dkvw, mate_dkv, far_src, far_in, near_src, near_in, dkv_x, dq_x, d3,
     g_src, g_mine, g_core, g_c, g_y, g_zs, g_z, g_oy, g_oc,
     t_c, t_y, t_z, t_x, in_sem, send_sem, recv_sem,
 ):
@@ -138,7 +141,7 @@
         return (seq + o >= 0) & (seq + o < NSEQ)
 
     expected = len(greet)
-    for o in WIN_OFFSETS:
+    for o in CHIP_STEPS:
         @pl.when(seq_in(o))
         def _():
             pl.semaphore_signal(
@@ -226,9 +229,18 @@
         @pl.when((tile < 0) | (tile >= 2 * NSEQ))
         def _():
             kvw[t] = jnp.zeros((128, 256), BF16)
-            dkv_in[t] = jnp.zeros((128, 256), BF16)
 
     w_copy.wait()
+
+    zero_tile = jnp.zeros((2, 128, 256), BF16)
+    dkvw[17] = jnp.zeros((128, 256), BF16)
+    mate_dkv[0] = zero_tile
+    mate_dkv[5] = zero_tile
+    for n, d in enumerate((1, -1)):
+        @pl.when(jnp.logical_not(chip_in(d)))
+        def _():
+            far_in[n] = zero_tile
+            near_in[n] = zero_tile
 
     def project(c):
         rows = fbuf[c]
@@ -390,8 +402,8 @@
     tt_buf[x] = tt_src[x]
 
     dq_acc = jnp.zeros((128, 128), F32)
-    dkv_get = {}
-    for slot in (0, 8, 1, 7, 2, 6, 3, 5, 4):
+
+    def backward_slot(slot, dq_acc):
         for t in (2 * slot, 2 * slot + 1):
             if t >= NWIN:
                 continue
@@ -405,20 +417,55 @@
             dkvw[t, :, 0:128] = (dot_nn(ds, q_tile) * FACTOR).astype(BF16)
             dkvw[t, :, 128:256] = dot_nt(e0b, gb).astype(BF16)
             dq_acc = dq_acc + dot_tn(ds, kvw[t, :, 0:128])
-        o = slot - 4
-        if o != 0:
-            n = WIN_OFFSETS.index(o)
-            count = 1 if o == 4 else 2
-            dkv_get[4 - o] = remote(
-                dkvw.at[pl.ds(2 * slot, count)],
-                dkv_in.at[pl.ds(2 * (4 - o), count)],
-                S_DKV + n,
-                at_seq(o),
-                seq_in(o),
-                seq_in(-o),
+        return dq_acc
+
+    mate_in = {}
+    for slot in (1, 7, 3, 5):
+        dq_acc = backward_slot(slot, dq_acc)
+        j = slot // 2
+        mate_in[j] = remote(
+            dkvw.at[pl.ds(2 * slot, 2)], mate_dkv.at[j + 1], S_DKV + j, sibling
+        )
+
+    def chip_sum(e, t):
+        return dkvw[4 * e + t].astype(F32) + mate_dkv[e + core, t].astype(F32)
+
+    dq_acc = backward_slot(0, dq_acc)
+    dq_acc = backward_slot(8, dq_acc)
+    mate_in[0].wait_recv()
+    mate_in[3].wait_recv()
+    far = {}
+    for t in range(2):
+        for n, (e, d) in enumerate(((0, -1), (4, 1))):
+            far_src[n, t] = chip_sum(e, t).astype(BF16)
+            far[n, t] = remote(
+                far_src.at[n, t],
+                far_in.at[n, t],
+                S_DFAR + 2 * t + n,
+                at_seq(2 * d),
+                chip_in(2 * d),
+                chip_in(1) & chip_in(-1),
             )
+    for slot in (2, 6, 4):
+        dq_acc = backward_slot(slot, dq_acc)
     dq_x[x] = (dq_acc * FACTOR).astype(BF16)
     xq_in = [remote(dq_x.at[x], dq_x.at[x], S_XQ + k - 1, at_x(k)) for k in (1, 2, 3)]
+
+    mate_in[1].wait_recv()
+    mate_in[2].wait_recv()
+    near = {}
+    for t in range(2):
+        for n, (e, d) in enumerate(((1, -1), (3, 1))):
+            far[n, t].wait_recv()
+            near_src[n, t] = (chip_sum(e, t) + far_in[n, t].astype(F32)).astype(BF16)
+            near[n, t] = remote(
+                near_src.at[n, t],
+                near_in.at[n, t],
+                S_DNEAR + 2 * t + n,
+                at_seq(2 * d),
+                chip_in(d),
+                chip_in(-d),
+            )
 
     for copy in tt_in:
         copy.wait_recv()
@@ -446,25 +493,30 @@
         r, h = piece // 2, piece % 2
         att_out[128 * r : 128 * r + 128, 128 * h : 128 * h + 128] = att_buf[piece]
 
-    for slot in (4, 3, 5, 2, 6, 1, 7, 0, 8):
-        if slot != 4:
-            dkv_get[slot].wait_recv()
-    for t in range(2):
-        acc = dkvw[8 + t].astype(F32)
-        for slot in (3, 5, 2, 6, 1, 7, 0, 8):
-            if slot == 0 and t == 1:
-                continue
-            acc = acc + dkv_in[2 * slot + t].astype(F32)
+    xkv_in = []
+    for t in range(2):
+        for n in range(2):
+            near[n, t].wait_recv()
+        acc = chip_sum(2, t) + near_in[0, t].astype(F32) + near_in[1, t].astype(F32)
         dkv_x[x, t] = acc.astype(BF16)
-    xkv_in = [remote(dkv_x.at[x], dkv_x.at[x], S_XKV + k - 1, at_x(k)) for k in (1, 2, 3)]
+        xkv_in.append(
+            [
+                remote(
+                    dkv_x.at[x, t], dkv_x.at[x, t], (S_XKV, S_XKV2)[t] + k - 1, at_x(k)
+                )
+                for k in (1, 2, 3)
+            ]
+        )
 
     tc_in.wait_recv()
     t_y[y] = t_c[0] + t_c[1]
     ty_in = [remote(t_y.at[y], t_y.at[y], S_TY + k - 1, at_y(k)) for k in (1, 2, 3)]
 
-    for copy in xq_in + xkv_in:
-        copy.wait_recv()
-    for t in range(2):
+    for copy in xq_in:
+        copy.wait_recv()
+    for t in range(2):
+        for copy in xkv_in[t]:
+            copy.wait_recv()
         at_rows = slice(128 * t, 128 * t + 128)
         for h in range(2):
             d3[0, at_rows, 128 * h : 128 * h + 128] = dq_x[2 * t + h]
@@ -584,7 +636,11 @@
         pltpu.VMEM((4, TPAD, 128), F32),
         pltpu.VMEM((4, TPAD, 128), F32),
         pltpu.VMEM((18, 128, 256), BF16),
-        pltpu.VMEM((18, 128, 256), BF16),
+        pltpu.VMEM((6, 2, 128, 256), BF16),
+        pltpu.VMEM((2, 2, 128, 256), BF16),
+        pltpu.VMEM((2, 2, 128, 256), BF16),
+        pltpu.VMEM((2, 2, 128, 256), BF16),
+        pltpu.VMEM((2, 2, 128, 256), BF16),
         pltpu.VMEM((4, 2, 128, 256), BF16),
         pltpu.VMEM((4, 128, 128), BF16),
         pltpu.VMEM((2, 256, 384), BF16),

time: 88.6 us -> 84.9 us (0.958)
  Pallas kernels: 87.2 us -> 83.4 us
    pallas_call x1, Pallas kernels: 85.3 us -> 81.5 us  [local(): pl.pallas_call(kernel, out_shape=(jax.ShapeDtypeStruct((256, 256), BF16),...]
where the time goes in v4:
time: 84.9 us; the launch traced here: 84.7 us
  Pallas kernels  83.4 us (98%)
  between operations  1.29 us (2%)
    pallas_call x1, Pallas kernels, local(): pl.pallas_call(kernel, out_shape=(jax.ShapeDtypeStruct((256, 256), BF16),...  81.5 us
    pallas_call x1, Pallas kernels, local(): pl.pallas_call(finish, out_shape=(jax.ShapeDtypeStruct((1, 256, 256), BF1...  1.92 us

profile of v4, /device:TPU:1, one launch (start us, length us, event | category | flops | bytes accessed | tf_op | source)
XLA Modules:
  0.0 84.7 jit_solution(6623889872676463871)
XLA Ops:
  1.3 81.5 %shard_map.85 = (bf16[256,256]{1,0:T(8,128)(2,1)}, bf16[2,4,48,384]{3,2,1,0:T(8,128)(2,1)}, f32[32,128]{1,0:T(8,128)}) custom-call(bf16[192,256]{1,0:T(8,128)(2,1)} %bitcast.3, bf16[1536,768]{1,0:T(8,128)(2,1)} %w_hbm.1, s32[1,2,16]{2,1,0:T(2,128)} %buckets_ref.1, s32[1]{0:T(128)S(6)} %copy.9.ids_ref, f32[32,2,32]{2,1,0:T(2,128)} %bitcast.4, ...), custom_call_target="tpu_custom_call" | custom-call | tf_op jit(solution)/shard_map/pallas_call | solution.py:664
  82.8 1.9 %shard_map.86 = (bf16[1,256,256]{2,1,0:T(8,128)(2,1)}, f32[192,768]{1,0:T(8,128)}, f32[32,2,32]{2,1,0:T(2,128)}) custom-call(bf16[256,256]{1,0:T(8,128)(2,1)} %get-tuple-element.9.att_ref, bf16[2,4,48,384]{3,2,1,0:T(8,128)(2,1)} %get-tuple-element.10.pieces_ref, f32[32,128]{1,0:T(8,128)} %get-tuple-element.11.table_ref), custom_call_target="tpu_custom_call" | custom-call | tf_op jit(solution)/shard_map/pallas_call | solution.py:676

commit v5 on v4

--- a/solution.py
+++ b/solution.py
@@ -46,7 +46,11 @@
 S_XKV2 = 84
 S_DNEAR = 87
 S_DFAR = 91
-N_SEM = 95
+S_FWD = 95
+S_GY2 = 98
+S_OC2 = 101
+S_TCROSS = 104
+N_SEM = 105
 
 CHIP_STEPS = (-2, 2)
 
@@ -92,7 +96,7 @@
     ft_ref, feat_ref, dout_ref, tbl_ref, row_buf, oh_buf, bias_ref, w_ref, fbuf, fcross, dot_src, dot_buf, bias_buf, proj_kv, proj_q, q_buf, kvw,
     e0_buf, o_buf, m_buf, l_buf, d_buf, w_buf, dof_buf,
     att_src, att_buf, tt_src, tt_buf, dkvw, mate_dkv, far_src, far_in, near_src, near_in, dkv_x, dq_x, d3,
-    g_src, g_mine, g_core, g_c, g_y, g_zs, g_z, g_oy, g_oc,
+    g_src, g_core, g_c, g_y, g_zs, g_z, g_oy, g_oc,
     t_c, t_y, t_z, t_x, in_sem, send_sem, recv_sem,
 ):
     cell = lax.axis_index("cell")
@@ -112,15 +116,19 @@
     def at_cross(k):
         return ((1 - zh) * 4 + (x + k) % 4, seq)
 
+    antipode = at_cross(0)
+
+    def at_far(j):
+        return ((1 - zh) * 4 + x, ((z_lo + j) % 4) * 8 + y * 2 + core)
+
+    def at_near(j):
+        return (cell, ((z_lo + j) % 4) * 8 + y * 2 + core)
+
     def at_seq(o):
         return (cell, (seq + o + NSEQ) % NSEQ)
 
     def at_y(k):
         return (cell, z_lo * 8 + ((y + k) % 4) * 2 + core)
-
-    def at_z(k):
-        there = (zi + k) % 8
-        return ((there // 4) * 4 + x, (there % 4) * 8 + y * 2 + core)
 
     sibling = (cell, seq + 1 - 2 * core)
 
@@ -129,7 +137,8 @@
     barrier = pltpu.get_barrier_semaphore()
     greet = [at_cross(k) for k in range(4)] + [at_x(k) for k in (1, 2, 3)]
     greet += [sibling]
-    greet += [at_y(k) for k in (1, 2, 3)] + [at_z(k) for k in range(1, 8)]
+    greet += [at_y(k) for k in (1, 2, 3)] + [at_near(j) for j in (1, 2, 3)]
+    greet += [at_far(j) for j in (1, 2, 3)]
     for peer in greet:
         pl.semaphore_signal(barrier, inc=1, device_id=peer, device_id_type=pl.DeviceIdType.MESH)
     chip = seq // 2
@@ -218,7 +227,7 @@
         there = (x + k) % 4
         do_in.append(remote(dot_src.at[there], dot_buf.at[x], S_DO + k - 1, at_x(k)))
         bias_in.append(remote(bias_ref.at[there], bias_buf.at[x], S_BIAS + k - 1, at_x(k)))
-    cross_in = remote(ft_ref, fcross, S_FCROSS, at_cross(0))
+    cross_in = remote(ft_ref, fcross, S_FCROSS, antipode)
 
     dot_buf[x] = dot_src[x]
     bias_buf[x] = bias_ref[x]
@@ -242,19 +251,22 @@
             far_in[n] = zero_tile
             near_in[n] = zero_tile
 
-    def project(c):
-        rows = fbuf[c]
+    def project(c, rows):
         low = pl.multiple_of(192 * c, 64)
         tail = jnp.concatenate([rows[64:96, 0:64], rows[64:96, 64:128]], axis=0)
         return dot_nn(rows[0:64], w_ref[pl.ds(low, 128), :]) + dot_nn(
             tail, w_ref[pl.ds(pl.multiple_of(low + 128, 64), 64), :]
         )
 
-    proj = project(cell)
-    for z, k in ((0, 1), (0, 3), (0, 2), (1, 2), (1, 1), (1, 3), (1, 0)):
-        feat_in[z, k].wait_recv()
-        half_from = zh if z == 0 else 1 - zh
-        proj = proj + project(half_from * 4 + (x - k + 4) % 4)
+    proj = project(cell, fbuf[cell])
+    for k in (1, 3, 2):
+        feat_in[0, k].wait_recv()
+        c = zh * 4 + (x - k + 4) % 4
+        proj = proj + project(c, fbuf[c])
+    for k in (2, 1, 3, 0):
+        feat_in[1, k].wait_recv()
+        c = (1 - zh) * 4 + (x - k + 4) % 4
+        proj = proj + project(c, fbuf[c])
     projected = proj.astype(BF16)
     for h in range(2):
         proj_q[h] = projected[:, 128 * h : 128 * h + 128]
@@ -377,7 +389,6 @@
     m_all = m_buf[...]
     l_all = l_buf[...]
     big = jnp.zeros((TPAD, 128), F32)
-    att_in = []
     tt_in = []
     for c in range(4):
         z = m_all + bias_buf[c]
@@ -386,19 +397,12 @@
         mass = jnp.sum(ex * l_all, axis=0, keepdims=True)
         w_c = ex / mass
         w_buf[c] = w_c
-        acc = jnp.zeros((128, 128), F32)
-        for t in range(NWIN):
-            acc = acc + w_c[t : t + 1, :] * o_buf[t]
-        accb = acc.astype(BF16)
-        att_src[c] = acc.T.astype(BF16)
-        delta = jnp.sum(dof_buf[c] * accb.astype(F32), axis=0, keepdims=True)
+        delta = jnp.sum(w_c * d_buf[c], axis=0, keepdims=True)
         big = big + w_c * delta
         tt_src[c] = w_c * (d_buf[c] - delta * l_all)
     for k in (1, 2, 3):
         there = (x + k) % 4
-        att_in.append(remote(att_src.at[there], att_buf.at[x], S_ATT + k - 1, at_x(k)))
         tt_in.append(remote(tt_src.at[there], tt_buf.at[x], S_TT + k - 1, at_x(k)))
-    att_buf[x] = att_src[x]
     tt_buf[x] = tt_src[x]
 
     dq_acc = jnp.zeros((128, 128), F32)
@@ -467,6 +471,27 @@
                 chip_in(-d),
             )
 
+    for c in range(4):
+        acc = jnp.zeros((128, 128), F32)
+        for t in range(NWIN):
+            acc = acc + w_buf[c, t : t + 1, :] * o_buf[t]
+        att_src[c] = acc.T.astype(BF16)
+
+    xkv_in = []
+    for t in range(2):
+        for n in range(2):
+            near[n, t].wait_recv()
+        acc = chip_sum(2, t) + near_in[0, t].astype(F32) + near_in[1, t].astype(F32)
+        dkv_x[x, t] = acc.astype(BF16)
+        xkv_in.append(
+            [
+                remote(
+                    dkv_x.at[x, t], dkv_x.at[x, t], (S_XKV, S_XKV2)[t] + k - 1, at_x(k)
+                )
+                for k in (1, 2, 3)
+            ]
+        )
+
     for copy in tt_in:
         copy.wait_recv()
     ones = jnp.ones((8, 128), F32)
@@ -484,33 +509,8 @@
             )
         rows.append(row)
     both_heads = rows[0] + pltpu.roll(rows[1], 32, axis=1)
-    t_c[core] = hit * both_heads[0:1, :]
+    t_c[core] = both_heads
     tc_in = remote(t_c.at[core], t_c.at[core], S_TC, sibling)
-
-    for copy in att_in:
-        copy.wait_recv()
-    for piece in range(4):
-        r, h = piece // 2, piece % 2
-        att_out[128 * r : 128 * r + 128, 128 * h : 128 * h + 128] = att_buf[piece]
-
-    xkv_in = []
-    for t in range(2):
-        for n in range(2):
-            near[n, t].wait_recv()
-        acc = chip_sum(2, t) + near_in[0, t].astype(F32) + near_in[1, t].astype(F32)
-        dkv_x[x, t] = acc.astype(BF16)
-        xkv_in.append(
-            [
-                remote(
-                    dkv_x.at[x, t], dkv_x.at[x, t], (S_XKV, S_XKV2)[t] + k - 1, at_x(k)
-                )
-                for k in (1, 2, 3)
-            ]
-        )
-
-    tc_in.wait_recv()
-    t_y[y] = t_c[0] + t_c[1]
-    ty_in = [remote(t_y.at[y], t_y.at[y], S_TY + k - 1, at_y(k)) for k in (1, 2, 3)]
 
     for copy in xq_in:
         copy.wait_recv()
@@ -525,55 +525,72 @@
             d3[h, at_rows, 256 - 256 * h : 384 - 256 * h] = bothb[:, 0:128]
             d3[1, at_rows, 128 + 128 * h : 256 + 128 * h] = bothb[:, 128:256]
 
+    att_in = []
+    for k in (1, 2, 3):
+        there = (x + k) % 4
+        att_in.append(remote(att_src.at[there], att_buf.at[x], S_ATT + k - 1, at_x(k)))
+    att_buf[x] = att_src[x]
+
+    tc_in.wait_recv()
+    t_y[y] = t_c[0] + t_c[1]
+    ty_in = [remote(t_y.at[y], t_y.at[y], S_TY + k - 1, at_y(k)) for k in (1, 2, 3)]
+
     cross_in.wait_recv()
+    halves = ((1 - zh, fcross, S_GC, S_GY), (zh, ft_ref, S_GC2, S_GY2))
     theirs = d3[1 - core]
-    g_src[zh] = dot_nn(ft_ref[...], theirs).astype(BF16)
-    gc_in = [remote(g_src.at[zh], g_core.at[zh], S_GC, sibling)]
-    g_src[1 - zh] = dot_nn(fcross[...], theirs).astype(BF16)
-    gc_in.append(remote(g_src.at[1 - zh], g_core.at[1 - zh], S_GC2, sibling))
+    gc_in = []
+    for part, rows_ref, slot, _ in halves:
+        g_src[part] = dot_nn(rows_ref[...], theirs).astype(BF16)
+        gc_in.append(remote(g_src.at[part], g_core.at[part], slot, sibling))
     mine = d3[core]
-    g_mine[zh] = dot_nn(ft_ref[...], mine)
-    g_mine[1 - zh] = dot_nn(fcross[...], mine)
+    gy_in = []
+    for n, (part, rows_ref, _, slot) in enumerate(halves):
+        product = dot_nn(rows_ref[...], mine)
+        gc_in[n].wait_recv()
+        g_c[part] = (product + g_core[part].astype(F32)).astype(BF16)
+        for k in (1, 2, 3):
+            there = (y + k) % 4
+            gy_in.append(
+                remote(
+                    g_c.at[part, pl.ds(48 * there, 48)],
+                    g_y.at[y, part],
+                    slot + k - 1,
+                    at_y(k),
+                )
+            )
+        g_y[y, part] = g_c[part, pl.ds(48 * y, 48), :]
 
     for copy in ty_in:
         copy.wait_recv()
-    t_z[zi] = (t_y[0] + t_y[1]) + (t_y[2] + t_y[3])
-    tz_in = [remote(t_z.at[zi], t_z.at[zi], S_TZ + k - 1, at_z(k)) for k in range(1, 8)]
-
-    for copy in gc_in:
-        copy.wait_recv()
-    g_c[...] = (g_mine[...] + g_core[...].astype(F32)).astype(BF16)
-    gy_in = []
-    for k in (1, 2, 3):
-        there = (y + k) % 4
-        gy_in.append(
-            remote(g_c.at[:, pl.ds(48 * there, 48)], g_y.at[y], S_GY + k - 1, at_y(k))
-        )
-    g_y[y] = g_c[:, pl.ds(48 * y, 48), :]
+    t_z[z_lo] = (t_y[0] + t_y[1]) + (t_y[2] + t_y[3])
+    tz_in = [
+        remote(t_z.at[z_lo], t_z.at[z_lo], S_TZ + j - 1, at_near(j)) for j in (1, 2, 3)
+    ]
+    gz_in = []
+    for n, (part, _, _, _) in enumerate(halves):
+        for copy in gy_in[3 * n : 3 * n + 3]:
+            copy.wait_recv()
+        piece = g_y[0, part].astype(F32)
+        for k in (1, 2, 3):
+            piece = piece + g_y[k, part].astype(F32)
+        g_zs[part] = piece.astype(BF16)
+        for j in (0, 1, 3, 2) if n == 0 else (2, 1, 3):
+            peer = at_far(j) if n == 0 else at_near(j)
+            slot = S_GZ + j if n == 0 else S_GZ + 3 + j
+            gz_in.append(remote(g_zs.at[part], g_z.at[zi], slot, peer))
+    g_z[zi] = g_zs[zh]
 
     for copy in tz_in:
         copy.wait_recv()
-    total = t_z[0]
-    for k in range(1, 8):
-        total = total + t_z[k]
-    t_x[x] = total
-    tx_in = [remote(t_x.at[x], t_x.at[x], S_TX + k - 1, at_x(k)) for k in (1, 2, 3)]
-
-    for copy in gy_in:
-        copy.wait_recv()
-    piece = g_y[0].astype(F32)
-    for k in (1, 2, 3):
-        piece = piece + g_y[k].astype(F32)
-    g_zs[...] = piece.astype(BF16)
-    gz_in = []
-    for k in (4, 3, 5, 2, 6, 1, 7):
-        there = (zi + k) % 8
-        gz_in.append(remote(g_zs.at[there // 4], g_z.at[zi], S_GZ + k - 1, at_z(k)))
-    g_z[zi] = g_zs[zh]
+    sums = ((t_z[0] + t_z[1]) + (t_z[2] + t_z[3]))[0:1, :]
+    at_row = lax.broadcasted_iota(jnp.int32, (8, 128), 0)
+    at_type = (lax.broadcasted_iota(jnp.int32, (8, 128), 1) == ids_ref[0]).astype(F32)
+    t_x[zh, x] = jnp.where(at_row == 0, sums, jnp.where(at_row == 1, at_type, 0.0))
+    tx_in = [remote(t_x.at[zh, x], t_x.at[zh, x], S_TX + k - 1, at_x(k)) for k in (1, 2, 3)]
 
     for copy in tx_in:
         copy.wait_recv()
-    table_out[...] = (t_x[0] + t_x[1]) + (t_x[2] + t_x[3])
+    tcross_in = remote(t_x.at[zh], t_x.at[zh], S_TCROSS, antipode)
 
     for copy in gz_in:
         copy.wait_recv()
@@ -582,10 +599,28 @@
         piece = piece + g_z[k].astype(F32)
     g_oy[y] = piece.astype(BF16)
     oy_in = [remote(g_oy.at[y], g_oy.at[y], S_OY + k - 1, at_y(k)) for k in (1, 2, 3)]
-    for copy in oy_in:
-        copy.wait_recv()
-    oc_in = remote(g_oy, g_oc, S_OC, sibling)
-    oc_in.wait_recv()
+    oc_in = [remote(g_oy.at[y], g_oc.at[y], S_OC, sibling)]
+    for copy in att_in:
+        copy.wait_recv()
+    for piece in range(4):
+        r, h = piece // 2, piece % 2
+        att_out[128 * r : 128 * r + 128, 128 * h : 128 * h + 128] = att_buf[piece]
+
+    tcross_in.wait_recv()
+    cells = [t_x[c // 4, c % 4] for c in range(8)]
+    total = lax.dot_general(
+        jnp.concatenate([tile[1:2] for tile in cells], axis=0),
+        jnp.concatenate([tile[0:1] for tile in cells], axis=0),
+        (((0,), (0,)), ((), ())),
+        precision=lax.Precision.HIGHEST, preferred_element_type=F32,
+    )
+    table_out[...] = total[0:32]
+    for k in (1, 3, 2):
+        source = (y - k + 4) % 4
+        oy_in[k - 1].wait_recv()
+        oc_in.append(remote(g_oy.at[source], g_oc.at[source], S_OC2 + k - 1, sibling))
+    for copy in oc_in:
+        copy.wait_recv()
     grad_out[core] = g_oy[...]
     grad_out[1 - core] = g_oc[...]
     for copy in sends:
@@ -645,7 +680,6 @@
         pltpu.VMEM((4, 128, 128), BF16),
         pltpu.VMEM((2, 256, 384), BF16),
         pltpu.VMEM((2, 192, 384), BF16),
-        pltpu.VMEM((2, 192, 384), F32),
         pltpu.VMEM((2, 192, 384), BF16),
         pltpu.VMEM((2, 192, 384), BF16),
         pltpu.VMEM((4, 2, 48, 384), BF16),
@@ -653,10 +687,10 @@
         pltpu.VMEM((8, 48, 384), BF16),
         pltpu.VMEM((4, 48, 384), BF16),
         pltpu.VMEM((4, 48, 384), BF16),
-        pltpu.VMEM((2, 32, 128), F32),
-        pltpu.VMEM((4, 32, 128), F32),
-        pltpu.VMEM((8, 32, 128), F32),
-        pltpu.VMEM((4, 32, 128), F32),
+        pltpu.VMEM((2, 8, 128), F32),
+        pltpu.VMEM((4, 8, 128), F32),
+        pltpu.VMEM((4, 8, 128), F32),
+        pltpu.VMEM((2, 4, 8, 128), F32),
         pltpu.SemaphoreType.DMA((4,)),
         pltpu.SemaphoreType.DMA((N_SEM,)),
         pltpu.SemaphoreType.DMA((N_SEM,)),

time: 84.9 us -> 81.7 us (0.962)
  Pallas kernels: 83.4 us -> 79.4 us
    pallas_call x1, Pallas kernels: 81.5 us -> 77.5 us  [local(): pl.pallas_call(kernel, out_shape=(jax.ShapeDtypeStruct((256, 256), BF16),...]
where the time goes in v5:
time: 81.7 us; the launch traced here: 80.7 us
  Pallas kernels  79.4 us (97%)
  between operations  1.29 us (2%)
    pallas_call x1, Pallas kernels, local(): pl.pallas_call(kernel, out_shape=(jax.ShapeDtypeStruct((256, 256), BF16),...  77.5 us
    pallas_call x1, Pallas kernels, local(): pl.pallas_call(finish, out_shape=(jax.ShapeDtypeStruct((1, 256, 256), BF1...  1.92 us

profile of v5, /device:TPU:1, one launch (start us, length us, event | category | flops | bytes accessed | tf_op | source)
XLA Modules:
  0.0 80.7 jit_solution(2333356825609974455)
XLA Ops:
  1.3 77.5 %shard_map.85 = (bf16[256,256]{1,0:T(8,128)(2,1)}, bf16[2,4,48,384]{3,2,1,0:T(8,128)(2,1)}, f32[32,128]{1,0:T(8,128)}) custom-call(bf16[192,256]{1,0:T(8,128)(2,1)} %bitcast.3, bf16[1536,768]{1,0:T(8,128)(2,1)} %w_hbm.1, s32[1,2,16]{2,1,0:T(2,128)} %buckets_ref.1, s32[1]{0:T(128)S(6)} %copy.9.ids_ref, f32[32,2,32]{2,1,0:T(2,128)} %bitcast.4, ...), custom_call_target="tpu_custom_call" | custom-call | tf_op jit(solution)/shard_map/pallas_call | solution.py:698
  78.8 1.9 %shard_map.86 = (bf16[1,256,256]{2,1,0:T(8,128)(2,1)}, f32[192,768]{1,0:T(8,128)}, f32[32,2,32]{2,1,0:T(2,128)}) custom-call(bf16[256,256]{1,0:T(8,128)(2,1)} %get-tuple-element.9.att_ref, bf16[2,4,48,384]{3,2,1,0:T(8,128)(2,1)} %get-tuple-element.10.pieces_ref, f32[32,128]{1,0:T(8,128)} %get-tuple-element.11.table_ref), custom_call_target="tpu_custom_call" | custom-call | tf_op jit(solution)/shard_map/pallas_call | solution.py:710

commit v6 on v5

--- a/solution.py
+++ b/solution.py
@@ -227,7 +227,6 @@
         there = (x + k) % 4
         do_in.append(remote(dot_src.at[there], dot_buf.at[x], S_DO + k - 1, at_x(k)))
         bias_in.append(remote(bias_ref.at[there], bias_buf.at[x], S_BIAS + k - 1, at_x(k)))
-    cross_in = remote(ft_ref, fcross, S_FCROSS, antipode)
 
     dot_buf[x] = dot_src[x]
     bias_buf[x] = bias_ref[x]
@@ -273,6 +272,7 @@
         proj_kv[h, :, 0:128] = projected[:, 256 + 128 * h : 384 + 128 * h]
         proj_kv[h, :, 128:256] = projected[:, 512 + 128 * h : 640 + 128 * h]
 
+    cross_in = remote(ft_ref, fcross, S_FCROSS, antipode)
     my_tile = 8 + x // 2
     my_rows = pl.ds(64 * (x % 2), 64)
     kv_in = []
@@ -424,12 +424,16 @@
         return dq_acc
 
     mate_in = {}
-    for slot in (1, 7, 3, 5):
+    def to_mate(slot, dq_acc):
         dq_acc = backward_slot(slot, dq_acc)
         j = slot // 2
         mate_in[j] = remote(
             dkvw.at[pl.ds(2 * slot, 2)], mate_dkv.at[j + 1], S_DKV + j, sibling
         )
+        return dq_acc
+
+    dq_acc = to_mate(1, dq_acc)
+    dq_acc = to_mate(7, dq_acc)
 
     def chip_sum(e, t):
         return dkvw[4 * e + t].astype(F32) + mate_dkv[e + core, t].astype(F32)
@@ -450,6 +454,8 @@
                 chip_in(2 * d),
                 chip_in(1) & chip_in(-1),
             )
+    dq_acc = to_mate(3, dq_acc)
+    dq_acc = to_mate(5, dq_acc)
     for slot in (2, 6, 4):
         dq_acc = backward_slot(slot, dq_acc)
     dq_x[x] = (dq_acc * FACTOR).astype(BF16)
@@ -488,7 +494,7 @@
                 remote(
                     dkv_x.at[x, t], dkv_x.at[x, t], (S_XKV, S_XKV2)[t] + k - 1, at_x(k)
                 )
-                for k in (1, 2, 3)
+                for k in (2, 1, 3)
             ]
         )
 
@@ -548,7 +554,7 @@
         product = dot_nn(rows_ref[...], mine)
         gc_in[n].wait_recv()
         g_c[part] = (product + g_core[part].astype(F32)).astype(BF16)
-        for k in (1, 2, 3):
+        for k in (2, 1, 3):
             there = (y + k) % 4
             gy_in.append(
                 remote(

time: 81.7 us -> 78.8 us (0.965); the launches traced: 80.7 us -> 78.7 us
  Pallas kernels: 79.4 us -> 77.4 us
    pallas_call x1, Pallas kernels: 77.5 us -> 75.5 us  [local(): pl.pallas_call(kernel, out_shape=(jax.ShapeDtypeStruct((256, 256), BF16),...]
where the time goes in v6:
time: 78.8 us; the launch traced here: 78.7 us
  Pallas kernels  77.4 us (98%)
  between operations  1.29 us (2%)
    pallas_call x1, Pallas kernels, local(): pl.pallas_call(kernel, out_shape=(jax.ShapeDtypeStruct((256, 256), BF16),...  75.5 us
    pallas_call x1, Pallas kernels, local(): pl.pallas_call(finish, out_shape=(jax.ShapeDtypeStruct((1, 256, 256), BF1...  1.92 us

profile of v6, /device:TPU:1, one launch (start us, length us, event | category | flops | bytes accessed | tf_op | source)
XLA Modules:
  0.0 78.7 jit_solution(11786583462308980185)
XLA Ops:
  1.3 75.5 %shard_map.85 = (bf16[256,256]{1,0:T(8,128)(2,1)}, bf16[2,4,48,384]{3,2,1,0:T(8,128)(2,1)}, f32[32,128]{1,0:T(8,128)}) custom-call(bf16[192,256]{1,0:T(8,128)(2,1)} %bitcast.3, bf16[1536,768]{1,0:T(8,128)(2,1)} %w_hbm.1, s32[1,2,16]{2,1,0:T(2,128)} %buckets_ref.1, s32[1]{0:T(128)S(6)} %copy.9.ids_ref, f32[32,2,32]{2,1,0:T(2,128)} %bitcast.4, ...), custom_call_target="tpu_custom_call" | custom-call | tf_op jit(solution)/shard_map/pallas_call | solution.py:704
  76.8 1.9 %shard_map.86 = (bf16[1,256,256]{2,1,0:T(8,128)(2,1)}, f32[192,768]{1,0:T(8,128)}, f32[32,2,32]{2,1,0:T(2,128)}) custom-call(bf16[256,256]{1,0:T(8,128)(2,1)} %get-tuple-element.9.att_ref, bf16[2,4,48,384]{3,2,1,0:T(8,128)(2,1)} %get-tuple-element.10.pieces_ref, f32[32,128]{1,0:T(8,128)} %get-tuple-element.11.table_ref), custom_call_target="tpu_custom_call" | custom-call | tf_op jit(solution)/shard_map/pallas_call | solution.py:716
